TPU v7x, 512 devices: a whole 4x8x8 slice. The times are simulated.
512 devices in a mesh: tm: 64 (over z, x, core), band: 8 (over y).
Axes of the slice: x: 4, y: 8, z: 8, core: 2. Of those that a mesh axis runs over, the one named last changes fastest.
Arguments:
- query_input: bfloat16 [64, 40, 26, 1120], P('tm', 'band'), may hold values from -6 to 6
- key_input: bfloat16 [64, 40, 26, 1120], P('tm', 'band'), may hold values from -8 to 8
- value_input: bfloat16 [64, 40, 26, 1120], P('tm', 'band'), may hold values from -12 to 12
- cotangent: bfloat16 [64, 40, 26, 1120], P('tm', 'band'), may hold values from -6 to 6
- local_kernel_weight: float32 [3, 3, 1120], replicated, may hold values from -2 to 2
Outputs:
- mixed_out: bfloat16 [64, 40, 26, 1120], P('tm', 'band')
- query_grad: bfloat16 [64, 40, 26, 1120], P('tm', 'band')
- key_grad: bfloat16 [64, 40, 26, 1120], P('tm', 'band')
- value_grad: bfloat16 [64, 40, 26, 1120], P('tm', 'band')
- kernel_grad: float32 [3, 3, 1120], replicated
All inputs are finite; a program needn't handle non-finite values.
Results may differ from a plain program's by a relative error of at most 0.018.
Values may be sent and summed in bfloat16 or wider, within the bound.
No kernel may reach another device: no remote copies, remote signals or barrier semaphores. Data moves between devices by JAX's collectives and lax.ppermute only.
A program may use at most 128 MiB of HBM per device.

v0:
```python
import math

import jax
import jax.numpy as jnp
from jax import lax
from jax.sharding import PartitionSpec as P

HEADS = 35
HEAD_DIM = 32


def entering(shard, axis, combine, identity, reverse):
    devices, mine = (lax.axis_size(axis), lax.axis_index(axis))
    everything = jax.tree.map(lambda part: lax.all_gather(part, axis), shard)
    start = jax.tree.map(
        lambda part, zero: jnp.broadcast_to(jnp.asarray(zero, part.dtype), part.shape),
        shard,
        identity,
    )

    def step(k, before):
        at = devices - 1 - k if reverse else k
        reached = at > mine if reverse else at < mine
        new = combine(before, jax.tree.map(lambda part: part[at], everything))
        return jax.tree.map(lambda a, b: jnp.where(reached, a, b), new, before)

    return lax.fori_loop(0, devices, step, start)


def padded(cells, sides, width):
    for axis, dim in sides:
        count = lax.axis_size(axis)
        ends = count - 1
        head = lax.slice_in_dim(cells, 0, width, axis=dim)
        tail = lax.slice_in_dim(cells, cells.shape[dim] - width, cells.shape[dim], axis=dim)
        cells = jnp.concatenate(
            [
                lax.ppermute(tail, axis, [(i, (i + 1) % count) for i in range(ends)]),
                cells,
                lax.ppermute(head, axis, [((i + 1) % count, i) for i in range(ends)]),
            ],
            axis=dim,
        )
    return cells


def feature(x):
    return jnp.where(x > 0, x + 1.0, jnp.exp(jnp.minimum(x, 0.0)))


def slope(x):
    return jnp.where(x > 0, jnp.ones_like(x), jnp.exp(jnp.minimum(x, 0.0)))


def add_pair(earlier, later_term):
    return (earlier[0] + later_term[0], earlier[1] + later_term[1])


def frame_totals(terms, backward):
    frame = lax.psum(terms, "band")
    start = (jnp.zeros_like(frame[0]), jnp.zeros_like(frame[1]))
    before = entering(frame, "tm", add_pair, start, backward)
    return add_pair(before, frame)


def group_heads_count():
    chosen = 1
    for candidate in range(1, HEADS + 1):
        if HEADS % candidate == 0 and candidate * HEAD_DIM <= 256:
            chosen = candidate
    return chosen


def block_outer(left, right, group_count, group_heads, precise):
    count = left.shape[0]
    group_width = group_heads * HEAD_DIM
    left_groups = left.reshape(count, group_count, group_width)
    right_groups = right.reshape(count, group_count, group_width)
    if precise:
        whole = jnp.einsum(
            "tga,tgb->gab", left_groups, right_groups, precision=lax.Precision.HIGHEST
        )
    else:
        whole = jnp.einsum(
            "tga,tgb->gab", left_groups, right_groups, preferred_element_type=jnp.float32
        )
    whole = whole.reshape(group_count, group_heads, HEAD_DIM, group_heads, HEAD_DIM)
    same_head = jnp.eye(group_heads, dtype=jnp.float32)[None, :, None, :, None]
    return jnp.sum(whole * same_head, axis=3).reshape(HEADS, HEAD_DIM, HEAD_DIM)


def block_matrix(state, group_count, group_heads):
    group_width = group_heads * HEAD_DIM
    placed = state.reshape(group_count, group_heads, HEAD_DIM, 1, HEAD_DIM)
    same_head = jnp.eye(group_heads, dtype=jnp.float32)[None, :, None, :, None]
    return (placed * same_head).reshape(group_count, group_width, group_width)


def apply_blocks(rows, blocks, transposed):
    count = rows.shape[0]
    group_count, group_width = (blocks.shape[0], blocks.shape[1])
    grouped = rows.reshape(count, group_count, group_width)
    if transposed:
        result = jnp.einsum("tgb,gab->tga", grouped, blocks, precision=lax.Precision.HIGHEST)
    else:
        result = jnp.einsum("tga,gab->tgb", grouped, blocks, precision=lax.Precision.HIGHEST)
    return result.reshape(count, group_count * group_width)


def shards(query_input, key_input, value_input, cotangent, local_kernel_weight):
    high = lax.Precision.HIGHEST
    band_row_span, column_count, width = (
        query_input.shape[1],
        query_input.shape[2],
        query_input.shape[3],
    )
    count = band_row_span * column_count
    group_heads = group_heads_count()
    group_count = HEADS // group_heads
    indicator = (jnp.arange(width)[:, None] // HEAD_DIM == jnp.arange(HEADS)[None, :]).astype(
        jnp.float32
    )
    q_raw = query_input[0].reshape(count, width).astype(jnp.float32)
    k_raw = key_input[0].reshape(count, width).astype(jnp.float32)
    q_feat = feature(q_raw).astype(jnp.bfloat16)
    k_feat = feature(k_raw).astype(jnp.bfloat16)
    value_flat = value_input[0].reshape(count, width)
    own_state = block_outer(k_feat, value_flat, group_count, group_heads, False)
    own_norm = jnp.sum(k_feat, axis=0, dtype=jnp.float32).reshape(HEADS, HEAD_DIM)
    state, norm_vec = frame_totals((own_state, own_norm), False)
    q_wide = q_feat.astype(jnp.float32)
    state_blocks = block_matrix(state, group_count, group_heads)
    norm_flat = norm_vec.reshape(width)
    num = apply_blocks(q_wide, state_blocks, False)
    den = jnp.dot(q_wide * norm_flat, indicator, precision=high)
    den_wide = jnp.dot(den, indicator.T, precision=high)
    attn = num / den_wide
    stacked = jnp.stack([value_input[0], cotangent[0]])
    rimmed = padded(stacked, (("band", 1),), 1)
    padded_input = jnp.pad(rimmed, ((0, 0), (0, 0), (1, 1), (0, 0)))
    value_padded = padded_input[0]
    gpad = padded_input[1]
    complete_gradient = cotangent[0].astype(jnp.float32)
    local_output = jnp.zeros((band_row_span, column_count, width), jnp.float32)
    v_local = jnp.zeros((band_row_span, column_count, width), jnp.float32)
    kernel_row_slice = []
    for row_offset in range(3):
        for column_offset in range(3):
            local_output = (
                local_output
                + local_kernel_weight[row_offset, column_offset]
                * value_padded[
                    row_offset : row_offset + band_row_span,
                    column_offset : column_offset + column_count,
                ]
            )
            v_local = (
                v_local
                + local_kernel_weight[row_offset, column_offset]
                * gpad[
                    2 - row_offset : 2 - row_offset + band_row_span,
                    2 - column_offset : 2 - column_offset + column_count,
                ]
            )
            kernel_row_slice.append(
                jnp.sum(
                    complete_gradient
                    * value_padded[
                        row_offset : row_offset + band_row_span,
                        column_offset : column_offset + column_count,
                    ],
                    axis=(0, 1),
                )
            )
    mixed_out = (attn.reshape(band_row_span, column_count, width) + local_output).astype(
        jnp.bfloat16
    )[None]
    grad_flat = complete_gradient.reshape(count, width)
    scaled = grad_flat / den_wide
    den_grad = -jnp.dot(grad_flat * attn, indicator, precision=high) / den
    den_grad_wide = jnp.dot(den_grad, indicator.T, precision=high)
    back_state = block_outer(q_wide, scaled, group_count, group_heads, True)
    back_norm = jnp.sum(q_wide * den_grad_wide, axis=0).reshape(HEADS, HEAD_DIM)
    later_state, later_norm = frame_totals((back_state, back_norm), True)
    query_grad = apply_blocks(scaled, state_blocks, True) + den_grad_wide * norm_flat
    query_grad = (
        (query_grad * slope(q_raw))
        .reshape(band_row_span, column_count, width)
        .astype(jnp.bfloat16)[None]
    )
    later_blocks = block_matrix(later_state, group_count, group_heads)
    key_grad = apply_blocks(
        value_flat.astype(jnp.float32), later_blocks, True
    ) + later_norm.reshape(width)
    key_grad = (
        (key_grad * slope(k_raw))
        .reshape(band_row_span, column_count, width)
        .astype(jnp.bfloat16)[None]
    )
    value_grad = apply_blocks(k_feat.astype(jnp.float32), later_blocks, False)
    value_grad = (value_grad.reshape(band_row_span, column_count, width) + v_local).astype(
        jnp.bfloat16
    )[None]
    kernel_terms = jnp.stack(kernel_row_slice).reshape(3, 3, width)
    kernel_total = lax.psum(kernel_terms, ("tm", "band"))
    total_tokens = lax.axis_size("tm") * lax.axis_size("band") * count
    kernel_grad = kernel_total / math.sqrt(total_tokens)
    return (mixed_out, query_grad, key_grad, value_grad, kernel_grad)


def solution(mesh):
    placed = (
        P("tm", "band", None, None),
        P("tm", "band", None, None),
        P("tm", "band", None, None),
        P("tm", "band", None, None),
        P(),
    )
    return jax.shard_map(
        shards,
        mesh=mesh,
        in_specs=placed,
        out_specs=(
            P("tm", "band", None, None),
            P("tm", "band", None, None),
            P("tm", "band", None, None),
            P("tm", "band", None, None),
            P(),
        ),
        check_vma=False,
    )
```

profile of v0, /device:TPU:1, one launch (start us, length us, event | category | flops | bytes accessed | tf_op | source)
XLA Modules:
  0.0 863.7 jit_solution(13523367854085724787)
XLA Ops:
  10.0 2.6 reshape.180
  12.5 4.8 multiply_reduce_fusion.1
  17.4 79.9 %all-reduce.4.cloned.1.call-done = f32[35,32,32]{2,1,0:T(8,128)} async-done(((f32[35,32,32]{2,1,0:T(8,128)}), f32[35,32,32]{2,1,0:T(8,128)}) %all-reduce.4.cloned.1.call-update) | async-done | bytes 143376 | tf_op jit(solution)/shard_map/psum | solution.py:60
  97.5 22.3 %psum.36 = f32[35,32]{1,0:T(8,128)S(1)} all-reduce(f32[35,32]{1,0:T(8,128)S(1)} %reshape.182), channel_id=1, replica_groups=mesh['tm'=64,'band'=8] {'band'}, use_global_device_ids=true, to_apply=%region_3.4 | all-reduce | flops 1120 | bytes 8960 | tf_op jit(solution)/shard_map/psum | solution.py:60
  121.4 1.3 select_n.138
  123.8 69.4 %all-gather.4 = f32[64,35,32]{1,2,0:T(8,128)} all-gather(f32[1,35,32]{1,2,0:T(8,128)S(1)} %copy.44), channel_id=3, replica_groups=mesh['tm'=64,'band'=8] {'tm'}, dimensions={0}, use_global_device_ids=true | all-gather | bytes 291200 | tf_op jit(solution)/shard_map/all_gather | solution.py:14
  193.2 69.6 %all-gather.9.cloned.1.call-done = f32[2240,32,32]{2,1,0:T(8,128)} async-done(((f32[35,32,32]{2,1,0:T(8,128)}), f32[2240,32,32]{2,1,0:T(8,128)}) %all-gather.9.cloned.1.call-update) | async-done | bytes 9175056 | tf_op jit(solution)/shard_map/all_gather | solution.py:14
  262.8 135.1 %while.34 = (s32[]{:T(128)}, f32[35,32,32]{2,1,0:T(8,128)S(1)}, f32[35,32]{1,0:T(8,128)S(1)}, s32[]{:T(128)}, f32[64,35,32,32]{3,2,1,0:T(8,128)}, /*index=5*/f32[64,35,32]{1,2,0:T(8,128)}, s32[]{:T(128)}, s32[]{:T(128)}) while((s32[]{:T(128)}, f32[35,32,32]{2,1,0:T(8,128)S(1)}, f32[35,32]{1,0:T(8,128)S(1)}, s32[]{:T(128)}, ...), condition=%wide.region_5.6_spmd.clone, body=%wide.region_4.5_spmd.clone.sunk | while | flops 110884 | bytes 461555 | solution.py:27
  262.8 1.3 add_select_fusion.9
  264.9 1.3 add_select_fusion.9
  267.1 1.3 add_select_fusion.9
  269.2 1.3 add_select_fusion.9
  271.3 1.3 add_select_fusion.9
  273.4 1.3 add_select_fusion.9
  275.5 1.3 add_select_fusion.9
  277.6 1.3 add_select_fusion.9
  279.7 1.3 add_select_fusion.9
  281.8 1.3 add_select_fusion.9
  283.9 1.3 add_select_fusion.9
  286.0 1.3 add_select_fusion.9
  288.1 1.3 add_select_fusion.9
  290.3 1.3 add_select_fusion.9
  292.4 1.3 add_select_fusion.9
  294.5 1.3 add_select_fusion.9
  296.6 1.3 add_select_fusion.9
  298.7 1.3 add_select_fusion.9
  300.8 1.3 add_select_fusion.9
  302.9 1.3 add_select_fusion.9
  305.0 1.3 add_select_fusion.9
  307.1 1.3 add_select_fusion.9
  309.2 1.3 add_select_fusion.9
  311.4 1.3 add_select_fusion.9
  313.5 1.3 add_select_fusion.9
  315.6 1.3 add_select_fusion.9
  317.7 1.3 add_select_fusion.9
  319.8 1.3 add_select_fusion.9
  321.9 1.3 add_select_fusion.9
  398.0 2.4 mul.264
  400.4 3.6 mul.265
  405.9 2.4 reshape.183
  409.2 3.0 fusion.73
  412.2 1.5 reshape.185
  413.7 2.0 fusion.49
  415.7 3.9 reshape.187
  419.6 4.8 multiply_reduce_fusion
  424.4 70.0 %all-reduce.6.cloned.1.call-done = f32[35,32,32]{2,1,0:T(8,128)} async-done(((f32[35,32,32]{2,1,0:T(8,128)}), f32[35,32,32]{2,1,0:T(8,128)}) %all-reduce.6.cloned.1.call-update) | async-done | bytes 143376 | tf_op jit(solution)/shard_map/psum | solution.py:60
  494.6 3.2 collective-permute-start
  497.8 1.5 collective-permute-start.1
  499.3 2.0 select_n.142
  501.4 2.2 collective-permute-done.1
  503.6 1.5 fusion.10
  506.2 107.4 %psum.39 = f32[3,3,1120]{2,1,0:T(4,128)S(1)} all-reduce(f32[3,3,1120]{2,1,0:T(4,128)S(1)} %reshape.191), channel_id=1, replica_groups=mesh['tm'=64,'band'=8] {'tm','band'}, use_global_device_ids=true, to_apply=%region_21.22 | all-reduce | flops 10080 | bytes 80640 | tf_op jit(solution)/shard_map/psum | solution.py:205
  614.3 3.1 convolution_bitcast_fusion.3
  618.8 2.1 reshape.184
  620.9 2.2 fusion.4
  624.0 24.1 %psum.38 = f32[35,32]{1,0:T(8,128)S(1)} all-reduce(f32[35,32]{1,0:T(8,128)S(1)} %reshape.189), channel_id=1, replica_groups=mesh['tm'=64,'band'=8] {'band'}, use_global_device_ids=true, to_apply=%region_9.10 | all-reduce | flops 1120 | bytes 8960 | tf_op jit(solution)/shard_map/psum | solution.py:60
  649.0 58.1 %all-gather.5 = f32[64,35,32]{1,2,0:T(8,128)} all-gather(f32[1,35,32]{1,2,0:T(8,128)S(1)} %copy.52), channel_id=5, replica_groups=mesh['tm'=64,'band'=8] {'tm'}, dimensions={0}, use_global_device_ids=true | all-gather | bytes 291200 | tf_op jit(solution)/shard_map/all_gather | solution.py:14
  707.0 1.4 fusion.52
  708.4 135.5 %while.35 = (s32[]{:T(128)}, f32[35,32,32]{2,1,0:T(8,128)S(1)}, f32[35,32]{1,0:T(8,128)S(1)}, s32[]{:T(128)}, f32[64,35,32,32]{3,2,1,0:T(8,128)}, /*index=5*/f32...) while((s32[]{:T(128)}, f32[35,32,32]{2,1,0:T(8,128)S(1)}, ...), condition=%wide.region_11.12_spmd.clone, body=%wide.region_10.11_spmd.clone.sunk | while | flops 110888 | bytes 461617 | solution.py:27
  708.4 1.3 add_select_fusion.11
  844.0 2.4 mul.306
  846.4 3.6 mul.307
  851.1 1.8 convolution_bitcast_fusion.1
  854.8 1.4 fusion.53
  (592 shorter events, 246.8 us)
Async XLA Ops:
  7.2 1.8 copy-start.17
  7.2 90.1 %all-reduce.4.cloned.1.call-start = ((), (), s32[]{:S(2)}) async-start(), calls=%async_computation | async-start | bytes 1146880 | tf_op jit(solution)/shard_map/psum | solution.py:60
  9.0 1.0 copy-start.5
  9.5 3.0 copy-start.7
  17.4 245.4 %all-gather.9.cloned.1.call-start = ((), (), s32[]{:S(2)}) async-start(), calls=%async_computation.2 | async-start | bytes 37273600 | tf_op jit(solution)/shard_map/all_gather | solution.py:14
  97.3 22.9 %copy-start.20 = (bf16[1,5,26,1120]{3,2,1,0:T(8,128)(2,1)S(1)}, bf16[1,5,26,1120]{3,2,1,0:T(8,128)(2,1)}, u32[]{:S(2)}) copy-start(bf16[1,5,26,1120]{3,2,1,0:T(8,128)(2,1)} %param.9) | copy-start | bytes 873604
  97.3 397.1 %all-reduce.6.cloned.1.call-start = ((), (), s32[]{:S(2)}) async-start(), calls=%async_computation.1 | async-start | bytes 1146880 | tf_op jit(solution)/shard_map/psum | solution.py:60
  121.4 1.4 copy-start.3
  122.7 285.6 %copy-start.1 = (f32[130,1120]{1,0:T(8,128)}, f32[130,1120]{1,0:T(8,128)S(1)}, u32[]{:S(2)}) copy-start(f32[130,1120]{1,0:T(8,128)S(1)} %reshape.192) | copy-start | bytes 1747204
  262.8 135.1 %copy-start.16 = (f32[35,32,32]{2,1,0:T(8,128)S(1)}, f32[35,32,32]{2,1,0:T(8,128)}, u32[]{:S(2)}) copy-start(f32[35,32,32]{2,1,0:T(8,128)} %all-reduce.4.cloned.1.call-done) | copy-start | bytes 430084
  400.4 3.6 copy-start.9
  412.2 1.5 copy-start.10
  413.7 5.8 copy-start
  424.4 70.1 %copy-start.18 = (bf16[1,5,26,1120]{3,2,1,0:T(8,128)(2,1)S(1)}, bf16[1,5,26,1120]{3,2,1,0:T(8,128)(2,1)}, u32[]{:S(2)}) copy-start(bf16[1,5,26,1120]{3,2,1,0:T(8,128)(2,1)} %param.11) | copy-start | bytes 873604
  424.4 284.0 %all-gather.11.cloned.1.call-start = ((), (), s32[]{:S(2)}) async-start(), calls=%async_computation.3 | async-start | bytes 37273600 | tf_op jit(solution)/shard_map/all_gather | solution.py:14
  494.5 3.2 copy-start.12
  494.5 6.8 copy-start.21
  494.6 6.9 collective-permute-start
  497.8 5.9 collective-permute-start.1
  618.8 4.3 copy-start.2
  620.9 2.2 copy-start.13
  620.9 2.2 copy-start.14
  623.9 83.1 %copy-start.4 = (f32[5,26,1120]{2,1,0:T(8,128)S(1)}, f32[5,26,1120]{2,1,0:T(8,128)}, u32[]{:S(2)}) copy-start(f32[5,26,1120]{2,1,0:T(8,128)} %reshape.184) | copy-start | bytes 1747204
  708.4 135.5 %copy-start.15 = (f32[35,32,32]{2,1,0:T(8,128)S(1)}, f32[35,32,32]{2,1,0:T(8,128)}, u32[]{:S(2)}) copy-start(f32[35,32,32]{2,1,0:T(8,128)} %all-reduce.6.cloned.1.call-done) | copy-start | bytes 430084
  846.4 3.6 copy-start.6
  850.0 1.0 copy-start.8
  853.1 1.1 copy-start.11
  854.8 1.4 copy-start.19
Sparse Core Ops, SparseCore 0:
  17.5 79.7 all-reduce.3
  100.6 162.1 all-gather.8
  424.5 69.8 all-reduce.5
  497.6 161.7 all-gather.10
where the time goes:
time: 877 us; the launch traced here: 864 us
  blocking collectives  281 us (32%)
  waiting for transfers between devices  222 us (25%)
  other arithmetic  182 us (21%)
  local copies, waits for them, and re-layouts  141 us (16%)
  matrix products  15.3 us (2%)
  between operations  14.3 us (2%)
    select_n x256, other arithmetic, step(): return jax.tree.map(lambda a, b: jnp.where(reached, a, b), new, before)  163 us
    psum x2, waiting for transfers between devices, frame_totals(): frame = lax.psum(terms, 'band')  150 us
    all_gather x2, blocking collectives, entering(): everything = jax.tree.map(lambda part: lax.all_gather(part, axis), shard)  127 us
    psum x1, blocking collectives, shards(): kernel_total = lax.psum(kernel_terms, ('tm', 'band'))  107 us
    dynamic_slice x256, local copies, waits for them, and re-layouts, step(): new = combine(before, jax.tree.map(lambda part: part[at], everything))  104 us
    all_gather x2, waiting for transfers between devices, entering(): everything = jax.tree.map(lambda part: lax.all_gather(part, axis), shard)  69.6 us
    psum x2, blocking collectives, frame_totals(): frame = lax.psum(terms, 'band')  46.4 us
  transfers between devices with their start and end apart: 6, of which 4 were waited for; matrix products, arithmetic and copies ran while one was open for 2% of the time, Pallas kernels for 0%

commit v1 on v0

v1 whole, which is shorter than its diff:
```python
import math

import jax
import jax.numpy as jnp
from jax import lax
from jax.experimental import pallas as pl
from jax.experimental.pallas import tpu as pltpu
from jax.sharding import Mesh
from jax.sharding import PartitionSpec as P

HEADS = 35
HEAD_DIM = 32
LANES = 128
WIDTH = HEADS * HEAD_DIM
GROUPS = -(-WIDTH // LANES)
PAD = 32
CHUNKS = 16
SLOTS = 3
STATE_TILES = 4 * GROUPS
EXTRA = STATE_TILES // SLOTS

f32 = jnp.float32
bf16 = jnp.bfloat16


def span(group):
    start = group * LANES
    return start, min(LANES, WIDTH - start)


def dot(a, b):
    return lax.dot_general(a, b, (((1,), (0,)), ((), ())), preferred_element_type=f32)


def dot_nt(a, b):
    return lax.dot_general(a, b, (((1,), (1,)), ((), ())), preferred_element_type=f32)


def dot_tn(a, b):
    return lax.dot_general(a, b, (((0,), (0,)), ((), ())), preferred_element_type=f32)


def split(x):
    high = x.astype(bf16)
    return high, (x - high.astype(f32)).astype(bf16)


def same_head():
    rows = lax.broadcasted_iota(jnp.int32, (LANES, LANES), 0) // HEAD_DIM
    columns = lax.broadcasted_iota(jnp.int32, (LANES, LANES), 1) // HEAD_DIM
    return rows == columns


def lane_head():
    return lax.broadcasted_iota(jnp.int32, (HEAD_DIM, LANES), 1) // HEAD_DIM


def compact(full, heads):
    out = jnp.zeros((HEAD_DIM, LANES), f32)
    for k in range(LANES // HEAD_DIM):
        out = jnp.where(heads == k, full[k * HEAD_DIM : (k + 1) * HEAD_DIM], out)
    return out


def expand(blocks, same):
    return jnp.where(same, jnp.concatenate([blocks] * (LANES // HEAD_DIM), axis=0), 0.0)


def put_state(send, group, blocks):
    for k in range(4):
        tile = group * 4 + k
        send[tile // SLOTS, pl.ds(8 * (tile % SLOTS), 8), :] = blocks[8 * k : 8 * k + 8]


def get_state(received, group):
    tiles = [group * 4 + k for k in range(4)]
    return jnp.concatenate(
        [received[t // SLOTS, pl.ds(8 * (t % SLOTS), 8), :] for t in tiles], axis=0
    )


def extra_tile(group):
    return EXTRA + group // SLOTS, 8 * (group % SLOTS)


def tail_rows(group):
    return EXTRA + (GROUPS + group // SLOTS) // SLOTS, (
        8 * ((GROUPS + group // SLOTS) % SLOTS) + 2 * (group % SLOTS)
    )


def clear_extra(send):
    for piece in range(EXTRA, CHUNKS):
        send[piece] = jnp.zeros((8 * SLOTS, LANES), f32)


def fill_rows(scratch, ref, rows):
    scratch[...] = jnp.zeros_like(scratch)
    for r in range(rows):
        scratch[r, pl.ds(0, ref.shape[1]), pl.ds(0, WIDTH)] = ref[r]


def state_kernel(k_ref, v_ref, g_ref, send, first, last, k_s, v_s):
    rows, columns = k_ref.shape[0], k_ref.shape[1]
    for n, ref in enumerate((v_ref, g_ref)):
        first[n] = ref[0]
        last[n] = ref[rows - 1]
    fill_rows(k_s, k_ref, rows)
    fill_rows(v_s, v_ref, rows)
    clear_extra(send)
    heads = lane_head()
    token = lax.broadcasted_iota(jnp.int32, (rows, PAD, LANES), 1) < columns
    for group in range(GROUPS):
        lanes = pl.ds(group * LANES, LANES)
        k_raw = k_s[:, :, lanes].astype(f32)
        feat = jnp.where(k_raw > 0, k_raw + 1.0, jnp.exp(jnp.minimum(k_raw, 0.0)))
        feat = jnp.where(token, feat, 0.0).astype(bf16).reshape(rows * PAD, LANES)
        value = v_s[:, :, lanes].reshape(rows * PAD, LANES)
        put_state(send, group, compact(dot_tn(feat, value), heads))
        piece, row = extra_tile(group)
        send[piece, pl.ds(row, 1), :] = jnp.sum(feat.astype(f32), axis=0, keepdims=True)


def totals_kernel(received, pair, send):
    bands = received.shape[0] // 2
    for core in range(2):
        total = received[core * bands]
        for band in range(1, bands):
            total = total + received[core * bands + band]
        pair[core] = total
    whole = pair[0] + pair[1]
    for n in range(send.shape[0]):
        send[n] = whole


def prefix_kernel(place, received, pair, send):
    at = place[0]
    carry = jnp.zeros(pair.shape[1:], f32)
    for n in range(received.shape[0]):
        carry = carry + jnp.where(n < at, received[n], 0.0)
    first = carry + pair[0]
    second = first + pair[1]
    bands = send.shape[0] // 2
    for band in range(bands):
        send[band] = first
        send[bands + band] = second


def suffix_kernel(place, received, pair, send):
    at, piece = place[0], place[1]
    later = jnp.zeros(pair.shape[1:], f32)
    earlier = jnp.zeros(pair.shape[1:], f32)
    for n in range(received.shape[0]):
        later = later + jnp.where(n > at, received[n], 0.0)
        earlier = earlier + jnp.where(n < at, received[n], 0.0)
    row = lax.broadcasted_iota(jnp.int32, pair.shape[1:], 0)
    extra = (piece - EXTRA) * (8 * SLOTS) + row
    norm = jnp.logical_and(extra < 8 * GROUPS, row % 8 == 0)
    summed = jnp.logical_and(piece >= EXTRA, jnp.logical_not(norm))
    second = later + pair[1]
    first = second + pair[0]
    whole = first + earlier
    first = jnp.where(summed, whole, first)
    second = jnp.where(summed, whole, second)
    bands = send.shape[0] // 2
    for band in range(bands):
        send[band] = first
        send[bands + band] = second


def local_kernel(v_ref, g_ref, above, below, w_ref, local, v_local, terms, v_s, g_s):
    rows, columns = v_ref.shape[0], v_ref.shape[1]
    for n, (scratch, ref) in enumerate(((v_s, v_ref), (g_s, g_ref))):
        scratch[...] = jnp.zeros_like(scratch)
        scratch[0, pl.ds(0, columns), pl.ds(0, WIDTH)] = above[n]
        scratch[rows + 1, pl.ds(0, columns), pl.ds(0, WIDTH)] = below[n]
        for r in range(rows):
            scratch[r + 1, pl.ds(0, columns), pl.ds(0, WIDTH)] = ref[r]
    terms[...] = jnp.zeros_like(terms)
    for group in range(GROUPS):
        start, wide = span(group)
        lanes = pl.ds(start, LANES)

        def shifted(scratch):
            out = []
            for r in range(rows + 2):
                here = scratch[r, :, lanes].astype(f32)
                out.append((pltpu.roll(here, 1, 0), here, pltpu.roll(here, PAD - 1, 0)))
            return out

        taps = [
            [jnp.broadcast_to(w_ref[i, pl.ds(j, 1), lanes], (PAD, LANES)) for j in range(3)]
            for i in range(3)
        ]
        value = shifted(v_s)
        for r in range(rows):
            total = jnp.zeros((PAD, LANES), f32)
            for i in range(3):
                for j in range(3):
                    total = total + taps[i][j] * value[r + i][j]
            local[r, :, lanes] = total
        for i in range(3):
            for j in range(3):
                term = jnp.zeros((PAD, LANES), f32)
                for r in range(rows):
                    term = term + g_s[r + 1, :, lanes].astype(f32) * value[r + i][j]
                n = 1 + 3 * i + j
                terms[pl.ds(n, 1), lanes] = jnp.sum(term, axis=0, keepdims=True)
        grad = shifted(g_s)
        for r in range(rows):
            total = jnp.zeros((PAD, LANES), f32)
            for i in range(3):
                for j in range(3):
                    total = total + taps[i][j] * grad[r + 2 - i][2 - j]
            v_local[r, :, lanes] = total


def query_kernel(q_ref, g_ref, received, local, terms, send, mixed, q_grad, q_s, g_s):
    rows, columns = q_ref.shape[0], q_ref.shape[1]
    tokens = rows * PAD
    fill_rows(q_s, q_ref, rows)
    fill_rows(g_s, g_ref, rows)
    clear_extra(send)
    heads, same = lane_head(), same_head()
    ones = same.astype(f32).astype(bf16)
    lane = lax.broadcasted_iota(jnp.int32, (1, LANES), 1)
    for group in range(GROUPS):
        start, wide = span(group)
        lanes = pl.ds(start, LANES)
        q_raw = q_s[:, :, lanes].reshape(tokens, LANES).astype(f32)
        low = jnp.exp(jnp.minimum(q_raw, 0.0))
        feat = jnp.where(q_raw > 0, q_raw + 1.0, low).astype(bf16)
        slope = jnp.where(q_raw > 0, 1.0, low)
        grad = g_s[:, :, lanes].reshape(tokens, LANES)
        high, rest = split(expand(get_state(received, group), same))
        piece, row = extra_tile(group)
        norm = received[piece, pl.ds(row, 1), :]
        norm = jnp.where(lane < wide, norm, 1.0)
        num = dot(feat, high) + dot(feat, rest)
        wide_feat = feat.astype(f32)
        a, b = split(wide_feat * norm)
        inverse = 1.0 / (dot(a, ones) + dot(b, ones))
        attn = num * inverse
        a, b = split(grad.astype(f32) * num)
        along = (dot(a, ones) + dot(b, ones)) * inverse
        back = dot_nt(grad, high) + dot_nt(grad, rest)
        back = (back - along * norm) * inverse * slope
        scaled = wide_feat * inverse
        a, b = split(scaled)
        put_state(send, group, compact(dot_tn(grad, a) + dot_tn(grad, b), heads))
        block = terms[pl.ds(0, 16), lanes]
        back_norm = -jnp.sum(scaled * along, axis=0, keepdims=True)
        send[piece, pl.ds(row, 8), :] = block[0:8]
        send[piece, pl.ds(row, 1), :] = back_norm
        piece, row = tail_rows(group)
        send[piece, pl.ds(row, 2), :] = block[8:10]
        here = attn.reshape(rows, PAD, LANES) + local[:, :, lanes]
        mixed[:, :, pl.ds(start, wide)] = here[:, :columns, :wide].astype(bf16)
        back = back.reshape(rows, PAD, LANES)
        q_grad[:, :, pl.ds(start, wide)] = back[:, :columns, :wide].astype(bf16)


def key_kernel(scale, k_ref, v_ref, received, v_local, k_grad, v_grad, kernel_grad, k_s, v_s):
    rows, columns = k_ref.shape[0], k_ref.shape[1]
    tokens = rows * PAD
    fill_rows(k_s, k_ref, rows)
    fill_rows(v_s, v_ref, rows)
    same = same_head()
    for group in range(GROUPS):
        start, wide = span(group)
        lanes = pl.ds(start, LANES)
        k_raw = k_s[:, :, lanes].reshape(tokens, LANES).astype(f32)
        low = jnp.exp(jnp.minimum(k_raw, 0.0))
        feat = jnp.where(k_raw > 0, k_raw + 1.0, low).astype(bf16)
        slope = jnp.where(k_raw > 0, 1.0, low)
        value = v_s[:, :, lanes].reshape(tokens, LANES)
        high, rest = split(expand(get_state(received, group), same))
        piece, row = extra_tile(group)
        head_rows = received[piece, pl.ds(row, 8), :]
        back = dot(value, high) + dot(value, rest) + head_rows[0:1]
        back = (back * slope).reshape(rows, PAD, LANES)
        k_grad[:, :, pl.ds(start, wide)] = back[:, :columns, :wide].astype(bf16)
        here = (dot_nt(feat, high) + dot_nt(feat, rest)).reshape(rows, PAD, LANES)
        here = here + v_local[:, :, lanes]
        v_grad[:, :, pl.ds(start, wide)] = here[:, :columns, :wide].astype(bf16)
        piece, row = tail_rows(group)
        tail = received[piece, pl.ds(row, 2), :]
        for n in range(9):
            term = head_rows[n + 1 : n + 2] if n < 7 else tail[n - 7 : n - 6]
            kernel_grad[n // 3, pl.ds(n % 3, 1), pl.ds(start, wide)] = (term * scale)[:, :wide]


def call(body, out_shape, name, scratch=(), scalars=0, keep=()):
    def run(*args):
        specs = [
            pl.BlockSpec(memory_space=pltpu.SMEM if n < scalars else pltpu.VMEM)
            for n in range(len(args))
        ]
        args = [
            a if n < scalars else pltpu.with_memory_space_constraint(a, pltpu.VMEM)
            for n, a in enumerate(args)
        ]
        return pl.pallas_call(
            body,
            out_shape=[
                a if n in keep else pltpu.VMEM(a.shape, a.dtype) for n, a in enumerate(out_shape)
            ],
            in_specs=specs,
            out_specs=[pl.BlockSpec(memory_space=pltpu.VMEM)] * len(out_shape),
            scratch_shapes=scratch,
            name=name,
        )(*args)

    return run


def shards(query_input, key_input, value_input, cotangent, local_kernel_weight):
    q, k, v, g = (x[0] for x in (query_input, key_input, value_input, cotangent))
    rows, columns, width = q.shape
    shape = jax.ShapeDtypeStruct
    lanes = GROUPS * LANES
    piece = (8 * SLOTS, LANES)
    planes = lax.axis_size("z") * lax.axis_size("x")
    place = jnp.stack(
        [
            lax.axis_index("z") * lax.axis_size("x") + lax.axis_index("x"),
            lax.axis_index("c") * lax.axis_size("y") + lax.axis_index("y"),
        ]
    ).astype(jnp.int32)
    token_scratch = pltpu.VMEM((rows, PAD, lanes), bf16)
    rim_scratch = pltpu.VMEM((rows + 2, PAD, lanes), bf16)
    tokens = shape(q.shape, bf16)
    padded = shape((rows, PAD, lanes), f32)
    edge = shape((2, columns, width), bf16)
    pieces = shape((CHUNKS, *piece), f32)

    def exchange(x):
        return lax.all_to_all(x, ("c", "y"), 0, 0, tiled=True)

    def across_frames(send, body, name):
        received = exchange(send)
        pair, whole = call(
            totals_kernel, (shape((2, *piece), f32), shape((planes, *piece), f32)), "totals"
        )(received)
        gathered = lax.all_to_all(whole, ("z", "x"), 0, 0, tiled=True)
        (back,) = call(body, (pieces,), name, scalars=1)(place, gathered, pair)
        return exchange(back)

    send, first, last = call(state_kernel, (pieces, edge, edge), "state", [token_scratch] * 2)(
        k, v, g
    )
    ends = lax.axis_size("y") - 1
    above = lax.ppermute(last, "y", [(i, i + 1) for i in range(ends)])
    below = lax.ppermute(first, "y", [(i + 1, i) for i in range(ends)])
    weight = jnp.pad(local_kernel_weight, ((0, 0), (0, 0), (0, lanes - width)))
    state = across_frames(send, prefix_kernel, "prefix")
    local, v_local, terms = call(
        local_kernel, (padded, padded, shape((16, lanes), f32)), "local", [rim_scratch] * 2
    )(v, g, above, below, weight)
    send, mixed, q_grad = call(
        query_kernel, (pieces, tokens, tokens), "query", [token_scratch] * 2, keep=(1, 2)
    )(q, g, state, local, terms)
    later = across_frames(send, suffix_kernel, "suffix")
    count = rows * columns
    for axis in ("z", "x", "c", "y"):
        count = count * lax.axis_size(axis)
    scale = 1.0 / math.sqrt(count)

    def key_body(*refs):
        key_kernel(scale, *refs)

    k_grad, v_grad, kernel_grad = call(
        key_body,
        (tokens, tokens, shape(local_kernel_weight.shape, f32)),
        "key",
        [token_scratch] * 2,
        keep=(0, 1, 2),
    )(k, v, later, v_local)
    return (mixed[None], q_grad[None], k_grad[None], v_grad[None], kernel_grad)


def solution(mesh):
    torus = Mesh(mesh.devices.reshape(8, 4, 2, 8), ("z", "x", "c", "y"))
    tokens = P(("z", "x", "c"), "y", None, None)
    return jax.shard_map(
        shards,
        mesh=torus,
        in_specs=(tokens, tokens, tokens, tokens, P()),
        out_specs=(tokens, tokens, tokens, tokens, P()),
        check_vma=False,
    )
```

time: 877 us -> 128 us (0.15); the launches traced: 864 us -> 127 us
  blocking collectives: 281 us -> 66.7 us
  waiting for transfers between devices: 222 us -> 18.4 us
  other arithmetic: 182 us -> 0.59 us
  local copies, waits for them, and re-layouts: 141 us -> 6.85 us
  starting transfers between devices: 4.85 us -> 23.5 us
  matrix products: 15.3 us -> 0 us
  between operations: 14.3 us -> 0.73 us
  Pallas kernels: 0 us -> 10.3 us
    select_n x258 -> x0, other arithmetic: 164 us -> none  [the longest x256 163 us: step(): return jax.tree.map(lambda a, b: jnp.where(reached, a, b), new, before)]
    psum x3 -> x0, blocking collectives: 154 us -> none  [the longest x1 107 us: shards(): kernel_total = lax.psum(kernel_terms, ('tm', 'band'))]
    psum x2 -> x0, waiting for transfers between devices: 150 us -> none  [frame_totals(): frame = lax.psum(terms, 'band')]
    all_gather x2 -> x0, blocking collectives: 127 us -> none  [entering(): everything = jax.tree.map(lambda part: lax.all_gather(part, axis), shard)]
    dynamic_slice x256 -> x0, local copies, waits for them, and re-layouts: 104 us -> none  [step(): new = combine(before, jax.tree.map(lambda part: part[at], everything))]
    all_gather x2 -> x0, waiting for transfers between devices: 69.6 us -> none  [entering(): everything = jax.tree.map(lambda part: lax.all_gather(part, axis), shard)]
    all_to_all x0 -> x4, blocking collectives: none -> 66.7 us  [the longest x3 49.1 us: exchange(): return lax.all_to_all(x, ('c', 'y'), 0, 0, tiled=True)]
    all_to_all x0 -> x2, starting transfers between devices: none -> 19 us  [the longest x1 12 us: across_frames(): gathered = lax.all_to_all(whole, ('z', 'x'), 0, 0, tiled=True)]
  transfers between devices with their start and end apart: 6 -> 4, of which waited for: 4 -> 3; matrix products, arithmetic and copies ran while one was open for 2% -> 0% of each run, Pallas kernels for 0% -> 1%
where the time goes in v1:
time: 128 us; the launch traced here: 127 us
  blocking collectives  66.7 us (52%)
  starting transfers between devices  23.5 us (18%)
  waiting for transfers between devices  18.4 us (14%)
  Pallas kernels  10.3 us (8%)
  local copies, waits for them, and re-layouts  6.85 us (5%)
    all_to_all x3, blocking collectives, exchange(): return lax.all_to_all(x, ('c', 'y'), 0, 0, tiled=True)  49.1 us
    all_to_all x1, blocking collectives, across_frames(): gathered = lax.all_to_all(whole, ('z', 'x'), 0, 0, tiled=True)  17.6 us
    all_to_all x1, waiting for transfers between devices, across_frames(): gathered = lax.all_to_all(whole, ('z', 'x'), 0, 0, tiled=True)  13.1 us
    all_to_all x1, starting transfers between devices, across_frames(): gathered = lax.all_to_all(whole, ('z', 'x'), 0, 0, tiled=True)  12 us
    pallas_call x8, Pallas kernels, run(): pl.pallas_call(body, out_shape=[a if n in keep else pltpu.VMEM(a.shape, a...  10.3 us
    all_to_all x1, starting transfers between devices, exchange(): return lax.all_to_all(x, ('c', 'y'), 0, 0, tiled=True)  6.99 us
    unnamed x24, local copies, waits for them, and re-layouts  6.84 us
    ppermute x1, waiting for transfers between devices, shards(): above = lax.ppermute(last, 'y', [(i, i + 1) for i in range(ends)])  3.51 us
  transfers between devices with their start and end apart: 4, of which 3 were waited for; matrix products, arithmetic and copies ran while one was open for 0% of the time, Pallas kernels for 1%

profile of v1, /device:TPU:1, one launch (start us, length us, event | category | flops | bytes accessed | tf_op | source)
XLA Modules:
  0.0 127.1 jit_solution(9749266264910640408)
XLA Ops:
  0.6 0.0 copy-start
  0.6 1.0 copy-done
  1.6 0.0 copy-start.2
  1.6 1.0 copy-done.2
  2.6 0.0 copy-start.4
  2.6 1.0 copy-done.4
  3.6 0.5 state.1
  4.1 17.6 %all_to_all.30.received = f32[16,24,128]{2,1,0:T(8,128)S(1)} all-to-all(f32[16,24,128]{2,1,0:T(8,128)S(1)} %get-tuple-element.21), channel_id=1, replica_groups=mesh['z'=8,'x'=4,'c'=2,'y'=8] {'c','y'}, dimensions={0} | all-to-all | bytes 393216 | tf_op jit(solution)/shard_map/all_to_all | solution.py:338
  21.7 0.8 totals.2
  22.5 12.0 %all-to-all-start.1 = ((f32[32,24,128]{2,1,0:T(8,128)}), f32[32,24,128]{2,1,0:T(8,128)S(1)}, u32[]{:S(2)}, u32[]{:S(2)}) async-start(f32[32,24,128]{2,1,0:T(8,128)} %get-tuple-element.22), calls=%async_computation.1 | async-start | bytes 786432 | tf_op jit(solution)/shard_map/all_to_all | solution.py:345
  34.5 0.6 pad_add_fusion.place
  35.1 13.1 %all-to-all-done.1.received = f32[32,24,128]{2,1,0:T(8,128)S(1)} async-done(((f32[32,24,128]{2,1,0:T(8,128)}), f32[32,24,128]{2,1,0:T(8,128)S(1)}, u32[]{:S(2)}, u32[]{:S(2)}) %all-to-all-start.1) | async-done | bytes 393248 | tf_op jit(solution)/shard_map/all_to_all | solution.py:345
  48.2 0.0 copy-start.11
  48.2 0.0 copy-start.3
  48.2 1.5 %prefix.1 = f32[16,24,128]{2,1,0:T(8,128)} custom-call(s32[2]{0:T(128)} %pad_add_fusion.place, f32[32,24,128]{2,1,0:T(8,128)S(1)} %all-to-all-done.1.received, f32[2,24,128]{2,1,0:T(8,128)S(1)} %get-tuple-element.23.pair), custom_call_target="tpu_custom_call" | custom-call | tf_op jit(solution)/shard_map/prefix/pallas_call | solution.py:303
  49.7 0.0 copy-start.1
  49.7 7.0 %all-to-all-start.2 = ((f32[16,24,128]{2,1,0:T(8,128)}), f32[16,24,128]{2,1,0:T(8,128)S(1)}, u32[]{:S(2)}, u32[]{:S(2)}) async-start(f32[16,24,128]{2,1,0:T(8,128)} %prefix.1), calls=%async_computation.2 | async-start | bytes 393216 | tf_op jit(solution)/shard_map/all_to_all | solution.py:338
  56.7 3.3 %collective-permute-start = (bf16[2,26,1120]{2,1,0:T(8,128)(2,1)S(1)}, bf16[2,26,1120]{2,1,0:T(8,128)(2,1)S(1)}, u32[]{:S(2)}, u32[]{:S(2)}) collective-permute-start(bf16[2,26,1120]{2,1,0:T(8,128)(2,1)S(1)} %get-tuple-element.24), channel_id=1, source_target_pairs={{0,1},{1,2},{2,3},{3,4},{4,5},{5,6},{6,7},{8,9},{9,10},{10,11},{11... | collective-permute-start | bytes 349448 | tf_op jit(solution)/shard_map/ppermute | solution.py:353
  60.0 1.3 %collective-permute-start.1 = (bf16[2,26,1120]{2,1,0:T(8,128)(2,1)S(1)}, bf16[2,26,1120]{2,1,0:T(8,128)(2,1)S(1)}, u32[]{:S(2)}, u32[]{:S(2)}) collective-permute-start(bf16[2,26,1120]{2,1,0:T(8,128)(2,1)S(1)} %get-tuple-element.25), channel_id=1, source_target_pairs={{1,0},{2,1},{3,2},{4,3},{5,4},{6,5},{7,6},{9,8},{10,9},{11,10},{12... | collective-permute-start | bytes 349448 | tf_op jit(solution)/shard_map/ppermute | solution.py:354
  61.3 0.0 copy-done.11
  61.4 3.5 %collective-permute-done.above = bf16[2,26,1120]{2,1,0:T(8,128)(2,1)S(1)} collective-permute-done((bf16[2,26,1120]{2,1,0:T(8,128)(2,1)S(1)}, bf16[2,26,1120]{2,1,0:T(8,128)(2,1)S(1)}, u32[]{:S(2)}, u32[]{:S(2)}) %collective-permute-start) | collective-permute-done | bytes 116512 | tf_op jit(solution)/shard_map/ppermute | solution.py:353
  64.9 1.8 %collective-permute-done.1.below = bf16[2,26,1120]{2,1,0:T(8,128)(2,1)S(1)} collective-permute-done((bf16[2,26,1120]{2,1,0:T(8,128)(2,1)S(1)}, bf16[2,26,1120]{2,1,0:T(8,128)(2,1)S(1)}, u32[]{:S(2)}, u32[]{:S(2)}) %collective-permute-start.1) | collective-permute-done | bytes 116512 | tf_op jit(solution)/shard_map/ppermute | solution.py:354
  66.7 0.0 copy-done.3
  66.7 0.0 copy-done.1
  66.7 1.8 %local.1 = (f32[5,32,1152]{2,1,0:T(8,128)S(1)}, f32[5,32,1152]{2,1,0:T(8,128)S(1)}, f32[16,1152]{1,0:T(8,128)S(1)}) custom-call(bf16[5,26,1120]{2,1,0:T(8,128)(2,1)S(1)} %bitcast.14, bf16[5,26,1120]{2,1,0:T(8,128)(2,1)S(1)} %bitcast.11, bf16[2,26,1120]{2,1,0:T(8,128)(2,1)S(1)} %collective-permute-done.above, ...), custom_call_target="tpu_custom_call" | custom-call | tf_op jit(solution)/shard_map/local/pallas_call | solution.py:303
  68.5 0.0 copy-start.6
  68.5 0.9 copy-done.6
  69.3 0.0 copy-start.8
  69.3 0.9 copy-done.8
  70.2 0.0 all-to-all-done.2.received
  70.2 0.0 copy-start.9
  70.2 1.1 copy-done.9
  71.4 0.0 copy-start.10
  71.4 1.0 copy-done.10
  72.4 3.1 %query.1 = (f32[16,24,128]{2,1,0:T(8,128)S(1)}, bf16[5,26,1120]{2,1,0:T(8,128)(2,1)}, bf16[5,26,1120]{2,1,0:T(8,128)(2,1)}) custom-call(bf16[5,26,1120]{2,1,0:T(8,128)(2,1)S(1)} %bitcast.18, bf16[5,26,1120]{2,1,0:T(8,128)(2,1)S(1)} %bitcast.12, f32[16,24,128]{2,1,0:T(8,128)S(1)} %all-to-all-done.2.received, f32[5,32,1152]{2,1,0:T(8,128)S(1)} %copy-done.9, ...), custom_call_target="tpu_custom_call" | custom-call | tf_op jit(solution)/shard_map/query/pallas_call | solution.py:303
  75.5 16.5 %all_to_all.31.received = f32[16,24,128]{2,1,0:T(8,128)S(1)} all-to-all(f32[16,24,128]{2,1,0:T(8,128)S(1)} %get-tuple-element.30), channel_id=1, replica_groups=mesh['z'=8,'x'=4,'c'=2,'y'=8] {'c','y'}, dimensions={0} | all-to-all | bytes 393216 | tf_op jit(solution)/shard_map/all_to_all | solution.py:338
  92.0 0.0 copy-start.7
  92.1 17.6 %all_to_all.32.received = f32[32,24,128]{2,1,0:T(8,128)S(1)} all-to-all(f32[32,24,128]{2,1,0:T(8,128)S(1)} %get-tuple-element.31), channel_id=1, replica_groups=mesh['z'=8,'x'=4,'c'=2,'y'=8] {'z','x'}, dimensions={0} | all-to-all | bytes 786432 | tf_op jit(solution)/shard_map/all_to_all | solution.py:345
  109.6 0.0 copy-start.5
  109.6 0.9 suffix.1
  110.6 14.9 %all_to_all.33.refs_2_ = f32[16,24,128]{2,1,0:T(8,128)S(1)} all-to-all(f32[16,24,128]{2,1,0:T(8,128)S(1)} %suffix.1), channel_id=1, replica_groups=mesh['z'=8,'x'=4,'c'=2,'y'=8] {'c','y'}, dimensions={0} | all-to-all | bytes 393216 | tf_op jit(solution)/shard_map/all_to_all | solution.py:338
  125.5 0.0 copy-done.7
  125.5 0.0 copy-done.5
  125.5 1.6 %key.1 = (bf16[5,26,1120]{2,1,0:T(8,128)(2,1)}, bf16[5,26,1120]{2,1,0:T(8,128)(2,1)}, f32[3,3,1120]{2,1,0:T(4,128)}) custom-call(bf16[5,26,1120]{2,1,0:T(8,128)(2,1)S(1)} %bitcast.17, bf16[5,26,1120]{2,1,0:T(8,128)(2,1)S(1)} %bitcast.15, f32[16,24,128]{2,1,0:T(8,128)S(1)} %all_to_all.33.refs_2_, f32[5,32,1152]{2,1,0:T(8,128)S(1)} %copy-done.7), custom_call_target="tpu_custom_call" | custom-call | tf_op jit(solution)/shard_map/key/pallas_call | solution.py:303
  (2 shorter events, 0.1 us)
Async XLA Ops:
  0.6 1.0 copy-start
  1.6 1.0 copy-start.2
  2.6 1.0 copy-start.4
  22.5 25.7 %all-to-all-start.1 = ((f32[32,24,128]{2,1,0:T(8,128)}), f32[32,24,128]{2,1,0:T(8,128)S(1)}, u32[]{:S(2)}, u32[]{:S(2)}) async-start(f32[32,24,128]{2,1,0:T(8,128)} %get-tuple-element.22), calls=%async_computation.1 | async-start | bytes 786432 | tf_op jit(solution)/shard_map/all_to_all | solution.py:345
  48.2 13.1 %copy-start.11 = (f32[3,3,1120]{2,1,0:T(4,128)S(1)}, f32[3,3,1120]{2,1,0:T(4,128)}, u32[]{:S(2)}) copy-start(f32[3,3,1120]{2,1,0:T(4,128)} %param.9) | copy-start | bytes 120964
  48.2 18.5 %copy-start.3 = (bf16[1,5,26,1120]{3,2,1,0:T(8,128)(2,1)S(1)}, bf16[1,5,26,1120]{3,2,1,0:T(8,128)(2,1)}, u32[]{:S(2)}) copy-start(bf16[1,5,26,1120]{3,2,1,0:T(8,128)(2,1)} %param.7) | copy-start | bytes 873604
  49.7 16.9 %copy-start.1 = (bf16[1,5,26,1120]{3,2,1,0:T(8,128)(2,1)S(1)}, bf16[1,5,26,1120]{3,2,1,0:T(8,128)(2,1)}, u32[]{:S(2)}) copy-start(bf16[1,5,26,1120]{3,2,1,0:T(8,128)(2,1)} %param.8) | copy-start | bytes 873604
  49.7 20.5 %all-to-all-start.2 = ((f32[16,24,128]{2,1,0:T(8,128)}), f32[16,24,128]{2,1,0:T(8,128)S(1)}, u32[]{:S(2)}, u32[]{:S(2)}) async-start(f32[16,24,128]{2,1,0:T(8,128)} %prefix.1), calls=%async_computation.2 | async-start | bytes 393216 | tf_op jit(solution)/shard_map/all_to_all | solution.py:338
  56.7 8.1 %collective-permute-start = (bf16[2,26,1120]{2,1,0:T(8,128)(2,1)S(1)}, bf16[2,26,1120]{2,1,0:T(8,128)(2,1)S(1)}, u32[]{:S(2)}, u32[]{:S(2)}) collective-permute-start(bf16[2,26,1120]{2,1,0:T(8,128)(2,1)S(1)} %get-tuple-element.24), channel_id=1, source_target_pairs={{0,1},{1,2},{2,3},{3,4},{4,5},{5,6},{6,7},{8,9},{9,10},{10,11},{11... | collective-permute-start | bytes 349448 | tf_op jit(solution)/shard_map/ppermute | solution.py:353
  60.0 6.6 %collective-permute-start.1 = (bf16[2,26,1120]{2,1,0:T(8,128)(2,1)S(1)}, bf16[2,26,1120]{2,1,0:T(8,128)(2,1)S(1)}, u32[]{:S(2)}, u32[]{:S(2)}) collective-permute-start(bf16[2,26,1120]{2,1,0:T(8,128)(2,1)S(1)} %get-tuple-element.25), channel_id=1, source_target_pairs={{1,0},{2,1},{3,2},{4,3},{5,4},{6,5},{7,6},{9,8},{10,9},{11,10},{12... | collective-permute-start | bytes 349448 | tf_op jit(solution)/shard_map/ppermute | solution.py:354
  68.5 0.9 copy-start.6
  69.3 0.9 copy-start.8
  70.2 1.1 copy-start.9
  71.4 1.0 copy-start.10
  92.0 33.4 %copy-start.7 = (f32[5,32,1152]{2,1,0:T(8,128)S(1)}, f32[5,32,1152]{2,1,0:T(8,128)}, u32[]{:S(2)}) copy-start(f32[5,32,1152]{2,1,0:T(8,128)} %copy-done.6) | copy-start | bytes 2211844
  109.6 15.8 %copy-start.5 = (bf16[1,5,26,1120]{3,2,1,0:T(8,128)(2,1)S(1)}, bf16[1,5,26,1120]{3,2,1,0:T(8,128)(2,1)}, u32[]{:S(2)}) copy-start(bf16[1,5,26,1120]{3,2,1,0:T(8,128)(2,1)} %param.6) | copy-start | bytes 873604

commit v2 on v1

v2 whole, which is shorter than its diff:
```python
import math

import jax
import jax.numpy as jnp
from jax import lax
from jax.experimental import pallas as pl
from jax.experimental.pallas import tpu as pltpu
from jax.sharding import Mesh
from jax.sharding import PartitionSpec as P

HEADS = 35
HEAD_DIM = 32
LANES = 128
WIDTH = HEADS * HEAD_DIM
GROUPS = -(-WIDTH // LANES)
PAD = 32
STATE_ROWS = GROUPS * HEAD_DIM
TAIL_ROW = STATE_ROWS + 8 * GROUPS

f32 = jnp.float32
bf16 = jnp.bfloat16


def span(group):
    start = group * LANES
    return start, min(LANES, WIDTH - start)


def dot(a, b):
    return lax.dot_general(a, b, (((1,), (0,)), ((), ())), preferred_element_type=f32)


def dot_nt(a, b):
    return lax.dot_general(a, b, (((1,), (1,)), ((), ())), preferred_element_type=f32)


def dot_tn(a, b):
    return lax.dot_general(a, b, (((0,), (0,)), ((), ())), preferred_element_type=f32)


def split(x):
    high = x.astype(bf16)
    return high, (x - high.astype(f32)).astype(bf16)


def same_head():
    rows = lax.broadcasted_iota(jnp.int32, (LANES, LANES), 0) // HEAD_DIM
    columns = lax.broadcasted_iota(jnp.int32, (LANES, LANES), 1) // HEAD_DIM
    return rows == columns


def lane_head():
    return lax.broadcasted_iota(jnp.int32, (HEAD_DIM, LANES), 1) // HEAD_DIM


def compact(full, heads):
    out = jnp.zeros((HEAD_DIM, LANES), f32)
    for k in range(LANES // HEAD_DIM):
        out = jnp.where(heads == k, full[k * HEAD_DIM : (k + 1) * HEAD_DIM], out)
    return out


def expand(blocks, same):
    return jnp.where(same, jnp.concatenate([blocks] * (LANES // HEAD_DIM), axis=0), 0.0)


def state_rows(group):
    return pl.ds(group * HEAD_DIM, HEAD_DIM)


def norm_row(group):
    return pl.ds(STATE_ROWS + group, 1)


def head_rows(group, count=8):
    return pl.ds(STATE_ROWS + 8 * group, count)


def tail_rows(group):
    return pl.ds(TAIL_ROW + 2 * group, 2)


def clear_extra(send):
    send[pl.ds(STATE_ROWS, send.shape[0] - STATE_ROWS), :] = jnp.zeros(
        (send.shape[0] - STATE_ROWS, LANES), f32
    )


def fill_rows(scratch, ref, rows):
    scratch[...] = jnp.zeros_like(scratch)
    for r in range(rows):
        scratch[r, pl.ds(0, ref.shape[1]), pl.ds(0, WIDTH)] = ref[r]


def edge_kernel(row, v_ref, g_ref, out):
    for n, ref in enumerate((v_ref, g_ref)):
        out[n] = ref[row]


def state_kernel(k_ref, v_ref, send, k_s, v_s):
    rows, columns = k_ref.shape[0], k_ref.shape[1]
    fill_rows(k_s, k_ref, rows)
    fill_rows(v_s, v_ref, rows)
    clear_extra(send)
    heads = lane_head()
    token = lax.broadcasted_iota(jnp.int32, (rows, PAD, LANES), 1) < columns
    for group in range(GROUPS):
        lanes = pl.ds(group * LANES, LANES)
        k_raw = k_s[:, :, lanes].astype(f32)
        feat = jnp.where(k_raw > 0, k_raw + 1.0, jnp.exp(jnp.minimum(k_raw, 0.0)))
        feat = jnp.where(token, feat, 0.0).astype(bf16).reshape(rows * PAD, LANES)
        value = v_s[:, :, lanes].reshape(rows * PAD, LANES)
        send[state_rows(group), :] = compact(dot_tn(feat, value), heads)
        send[norm_row(group), :] = jnp.sum(feat.astype(f32), axis=0, keepdims=True)


def totals_kernel(received, frames, send):
    count = frames.shape[0]
    bands = received.shape[0] // count
    whole = jnp.zeros(received.shape[1:], f32)
    for frame in range(count):
        total = received[frame * bands]
        for band in range(1, bands):
            total = total + received[frame * bands + band]
        frames[frame] = total
        whole = whole + total
    for n in range(send.shape[0]):
        send[n] = whole


def prefix_kernel(received, frames, send):
    plane = lax.axis_index("z")
    total = jnp.zeros(received.shape[1:], f32)
    for n in range(received.shape[0]):
        total = total + jnp.where(n < plane, received[n], 0.0)
    count = frames.shape[0]
    bands = send.shape[0] // count
    for frame in range(count):
        total = total + frames[frame]
        for band in range(bands):
            send[frame * bands + band] = total


def suffix_kernel(received, frames, send):
    plane = lax.axis_index("z")
    later = jnp.zeros(received.shape[1:], f32)
    whole = jnp.zeros(received.shape[1:], f32)
    for n in range(received.shape[0]):
        later = later + jnp.where(n > plane, received[n], 0.0)
        whole = whole + received[n]
    lane = lax.broadcasted_iota(jnp.int32, received.shape[1:], 1)
    first = lax.axis_index(("x", "c", "y")) * (received.shape[2] // LANES)
    row = first + lane // LANES
    norm = jnp.logical_and(row < TAIL_ROW, (row - STATE_ROWS) % 8 == 0)
    summed = jnp.logical_and(row >= STATE_ROWS, jnp.logical_not(norm))
    count = frames.shape[0]
    bands = send.shape[0] // count
    for frame in reversed(range(count)):
        later = later + frames[frame]
        out = jnp.where(summed, whole, later)
        for band in range(bands):
            send[frame * bands + band] = out


def fill_rim(scratch, ref, above, below=None):
    rows, columns = ref.shape[0], ref.shape[1]
    scratch[...] = jnp.zeros_like(scratch)
    scratch[0, pl.ds(0, columns), pl.ds(0, WIDTH)] = above
    for r in range(rows):
        scratch[r + 1, pl.ds(0, columns), pl.ds(0, WIDTH)] = ref[r]
    if below is not None:
        scratch[rows + 1, pl.ds(0, columns), pl.ds(0, WIDTH)] = below


def shifted(scratch, lanes):
    out = []
    for r in range(scratch.shape[0]):
        here = scratch[r, :, lanes].astype(f32)
        out.append((pltpu.roll(here, 1, 0), here, pltpu.roll(here, PAD - 1, 0)))
    return out


def terms_kernel(v_ref, g_ref, above, terms, v_s, g_s):
    rows = v_ref.shape[0]
    fill_rim(v_s, v_ref, above[0])
    fill_rim(g_s, g_ref, above[1])
    terms[...] = jnp.zeros_like(terms)
    for group in range(GROUPS):
        lanes = pl.ds(group * LANES, LANES)
        value = shifted(v_s, lanes)
        grad = [g_s[r, :, lanes].astype(f32) for r in range(rows + 1)]
        for n in range(9):
            step = n // 3 - 1
            term = jnp.zeros((PAD, LANES), f32)
            for r in range(1 - max(step, 0), rows + 1 - max(step, 0)):
                term = term + grad[r] * value[r + step][n % 3]
            terms[pl.ds(1 + n, 1), lanes] = jnp.sum(term, axis=0, keepdims=True)


def attend(q_s, g_s, received, group, same, ones):
    tokens = q_s.shape[0] * PAD
    wide = span(group)[1]
    lanes = pl.ds(group * LANES, LANES)
    q_raw = q_s[:, :, lanes].reshape(tokens, LANES).astype(f32)
    low = jnp.exp(jnp.minimum(q_raw, 0.0))
    feat = jnp.where(q_raw > 0, q_raw + 1.0, low).astype(bf16)
    slope = jnp.where(q_raw > 0, 1.0, low)
    grad = g_s[:, :, lanes].reshape(tokens, LANES)
    state = split(expand(received[state_rows(group), :], same))
    norm = received[norm_row(group), :]
    norm = jnp.where(lax.broadcasted_iota(jnp.int32, (1, LANES), 1) < wide, norm, 1.0)
    num = dot(feat, state[0]) + dot(feat, state[1])
    a, b = split(feat.astype(f32) * norm)
    inverse = 1.0 / (dot(a, ones) + dot(b, ones))
    a, b = split(grad.astype(f32) * num)
    along = (dot(a, ones) + dot(b, ones)) * inverse
    return feat, slope, grad, state, norm, num, inverse, along


def query_kernel(q_ref, g_ref, received, terms, send, q_s, g_s):
    rows = q_ref.shape[0]
    fill_rows(q_s, q_ref, rows)
    fill_rows(g_s, g_ref, rows)
    clear_extra(send)
    heads, same = lane_head(), same_head()
    ones = same.astype(f32).astype(bf16)
    for group in range(GROUPS):
        feat, _, grad, _, _, _, inverse, along = attend(q_s, g_s, received, group, same, ones)
        scaled = feat.astype(f32) * inverse
        a, b = split(scaled)
        send[state_rows(group), :] = compact(dot_tn(grad, a) + dot_tn(grad, b), heads)
        lanes = pl.ds(group * LANES, LANES)
        send[head_rows(group, 8), :] = terms[pl.ds(0, 8), lanes]
        send[head_rows(group, 1), :] = -jnp.sum(scaled * along, axis=0, keepdims=True)
        send[tail_rows(group), :] = terms[pl.ds(8, 2), lanes]


def grad_kernel(q_ref, g_ref, received, q_grad, attn, q_s, g_s):
    rows, columns = q_ref.shape[0], q_ref.shape[1]
    fill_rows(q_s, q_ref, rows)
    fill_rows(g_s, g_ref, rows)
    same = same_head()
    ones = same.astype(f32).astype(bf16)
    for group in range(GROUPS):
        start, wide = span(group)
        _, slope, grad, state, norm, num, inverse, along = attend(
            q_s, g_s, received, group, same, ones
        )
        back = dot_nt(grad, state[0]) + dot_nt(grad, state[1])
        back = ((back - along * norm) * inverse * slope).reshape(rows, PAD, LANES)
        q_grad[:, :, pl.ds(start, wide)] = back[:, :columns, :wide].astype(bf16)
        attn[:, :, pl.ds(start, LANES)] = (num * inverse).reshape(rows, PAD, LANES)


def mixed_kernel(v_ref, g_ref, above, below, w_ref, attn, mixed, v_local, v_s, g_s):
    rows, columns = v_ref.shape[0], v_ref.shape[1]
    fill_rim(v_s, v_ref, above[0], below[0])
    fill_rim(g_s, g_ref, above[1], below[1])
    for group in range(GROUPS):
        start, wide = span(group)
        lanes = pl.ds(start, LANES)
        taps = [
            jnp.broadcast_to(w_ref[n // 3, pl.ds(n % 3, 1), lanes], (PAD, LANES)) for n in range(9)
        ]
        value, grads = shifted(v_s, lanes), shifted(g_s, lanes)
        for r in range(rows):
            here = jnp.zeros((PAD, LANES), f32)
            there = jnp.zeros((PAD, LANES), f32)
            for n, tap in enumerate(taps):
                here = here + tap * value[r + n // 3][n % 3]
                there = there + tap * grads[r + 2 - n // 3][2 - n % 3]
            v_local[r, :, lanes] = there
            here = attn[r, :, lanes] + here
            mixed[r, :, pl.ds(start, wide)] = here[:columns, :wide].astype(bf16)


def key_kernel(scale, k_ref, v_ref, received, v_local, k_grad, v_grad, kernel_grad, k_s, v_s):
    rows, columns = k_ref.shape[0], k_ref.shape[1]
    tokens = rows * PAD
    fill_rows(k_s, k_ref, rows)
    fill_rows(v_s, v_ref, rows)
    same = same_head()
    for group in range(GROUPS):
        start, wide = span(group)
        lanes = pl.ds(start, LANES)
        k_raw = k_s[:, :, lanes].reshape(tokens, LANES).astype(f32)
        low = jnp.exp(jnp.minimum(k_raw, 0.0))
        feat = jnp.where(k_raw > 0, k_raw + 1.0, low).astype(bf16)
        slope = jnp.where(k_raw > 0, 1.0, low)
        value = v_s[:, :, lanes].reshape(tokens, LANES)
        high, rest = split(expand(received[state_rows(group), :], same))
        ahead = received[head_rows(group), :]
        back = dot(value, high) + dot(value, rest) + ahead[0:1]
        back = (back * slope).reshape(rows, PAD, LANES)
        k_grad[:, :, pl.ds(start, wide)] = back[:, :columns, :wide].astype(bf16)
        here = (dot_nt(feat, high) + dot_nt(feat, rest)).reshape(rows, PAD, LANES)
        here = here + v_local[:, :, lanes]
        v_grad[:, :, pl.ds(start, wide)] = here[:, :columns, :wide].astype(bf16)
        tail = received[tail_rows(group), :]
        for n in range(9):
            term = ahead[n + 1 : n + 2] if n < 7 else tail[n - 7 : n - 6]
            kernel_grad[n // 3, pl.ds(n % 3, 1), pl.ds(start, wide)] = (term * scale)[:, :wide]


def call(body, out_shape, name, scratch=(), plain=(), keep=()):
    def run(*args):
        args = [
            a if n in plain else pltpu.with_memory_space_constraint(a, pltpu.VMEM)
            for n, a in enumerate(args)
        ]
        return pl.pallas_call(
            body,
            out_shape=[
                a if n in keep else pltpu.VMEM(a.shape, a.dtype) for n, a in enumerate(out_shape)
            ],
            in_specs=[pl.BlockSpec(memory_space=pltpu.VMEM)] * len(args),
            out_specs=[pl.BlockSpec(memory_space=pltpu.VMEM)] * len(out_shape),
            scratch_shapes=scratch,
            name=name,
        )(*args)

    return run


def shards(query_input, key_input, value_input, cotangent, local_kernel_weight):
    q, k, v, g = (x[0] for x in (query_input, key_input, value_input, cotangent))
    rows, columns, width = q.shape
    shape = jax.ShapeDtypeStruct
    lanes = GROUPS * LANES
    planes = lax.axis_size("z")
    frames = lax.axis_size("x") * lax.axis_size("c")
    peers = frames * lax.axis_size("y")
    token_scratch = pltpu.VMEM((rows, PAD, lanes), bf16)
    row_scratch = pltpu.VMEM((rows + 1, PAD, lanes), bf16)
    rim_scratch = pltpu.VMEM((rows + 2, PAD, lanes), bf16)
    tokens = shape(q.shape, bf16)
    padded = shape((rows, PAD, lanes), f32)
    edge_shape = shape((2, columns, width), bf16)

    def flat(rows_used):
        return shape((-(-rows_used // peers) * peers, LANES), f32)

    def exchange(x):
        return lax.all_to_all(x, ("x", "c", "y"), 0, 0, tiled=True)

    def scatter(send):
        return exchange(send.reshape(peers, 1, -1))

    def gather(received, body, name, beside, then):
        received, v_now, g_now = lax.optimization_barrier((received, v, g))
        piece = received.shape[1:]
        sums, whole = call(
            totals_kernel, (shape((frames, *piece), f32), shape((planes, *piece), f32)), "totals"
        )(received)
        gathered = lax.all_to_all(whole, "z", 0, 0, tiled=True)
        done = beside(v_now, g_now)
        gathered, done, then = lax.optimization_barrier((gathered, done, then))
        (back,) = call(body, (shape(received.shape, f32),), name)(gathered, sums)
        return exchange(back).reshape(-1, LANES), done, then

    def edge_rows(v, g, row):
        def body(*refs):
            edge_kernel(row, *refs)

        return call(body, (edge_shape,), "edge")(v, g)[0]

    ends = lax.axis_size("y") - 1
    upward = [(i, i + 1) for i in range(ends)]
    downward = [(i + 1, i) for i in range(ends)]
    (send,) = call(
        state_kernel, (flat(STATE_ROWS + GROUPS),), "state", [token_scratch] * 2, plain=(0, 1)
    )(k, v)
    def above_and_terms(v, g):
        above = lax.ppermute(edge_rows(v, g, rows - 1), "y", upward)
        return above, *call(terms_kernel, (shape((16, lanes), f32),), "terms", [row_scratch] * 2)(
            v, g, above
        )

    state, (above, terms), _ = gather(
        scatter(send), prefix_kernel, "prefix", above_and_terms, ()
    )
    (send,) = call(
        query_kernel, (flat(STATE_ROWS + 10 * GROUPS),), "query", [token_scratch] * 2
    )(q, g, state, terms)
    later, _, (q_late, v_late, g_late, state) = gather(
        scatter(send), suffix_kernel, "suffix", lambda v, g: (), (q, v, g, state)
    )
    below = lax.ppermute(edge_rows(v_late, g_late, 0), "y", downward)
    weight = jnp.pad(local_kernel_weight, ((0, 0), (0, 0), (0, lanes - width)))
    q_grad, attn = call(grad_kernel, (tokens, padded), "grad", [token_scratch] * 2, keep=(0,))(
        q_late, g_late, state
    )
    mixed, v_local = call(
        mixed_kernel, (tokens, padded), "mixed", [rim_scratch] * 2, keep=(0,)
    )(v_late, g_late, above, below, weight, attn)
    count = rows * columns
    for axis in ("z", "x", "c", "y"):
        count = count * lax.axis_size(axis)
    scale = 1.0 / math.sqrt(count)

    def key_body(*refs):
        key_kernel(scale, *refs)

    k_grad, v_grad, kernel_grad = call(
        key_body,
        (tokens, tokens, shape(local_kernel_weight.shape, f32)),
        "key",
        [token_scratch] * 2,
        keep=(0, 1, 2),
    )(k, v, later, v_local)
    return (mixed[None], q_grad[None], k_grad[None], v_grad[None], kernel_grad)


def solution(mesh):
    torus = Mesh(mesh.devices.reshape(8, 4, 2, 8), ("z", "x", "c", "y"))
    tokens = P(("z", "x", "c"), "y", None, None)
    return jax.shard_map(
        shards,
        mesh=torus,
        in_specs=(tokens, tokens, tokens, tokens, P()),
        out_specs=(tokens, tokens, tokens, tokens, P()),
        check_vma=False,
    )
```

time: 128 us -> 111 us (0.87)
  waiting for transfers between devices: 18.4 us -> 11.2 us
  local copies, waits for them, and re-layouts: 6.85 us -> 0.04 us
  starting transfers between devices: 23.5 us -> 21.2 us
  blocking collectives: 66.7 us -> 64.6 us
  Pallas kernels: 10.3 us -> 12.4 us
    all_to_all x2, waiting for transfers between devices: 13.1 us -> 5.87 us  [the longest x1 5.87 us: gather(): gathered = lax.all_to_all(whole, 'z', 0, 0, tiled=True)]
    unnamed x24 -> x10, local copies, waits for them, and re-layouts: 6.84 us -> 0.02 us
    all_to_all x4, blocking collectives: 66.7 us -> 64.6 us  [the longest x3 55.5 us: exchange(): return lax.all_to_all(x, ('x', 'c', 'y'), 0, 0, tiled=True)]
    pallas_call x8 -> x12, Pallas kernels: 10.3 us -> 12.4 us  [run(): pl.pallas_call(body, out_shape=[a if n in keep else pltpu.VMEM(a.shape, a...]
    all_to_all x2, starting transfers between devices: 19 us -> 17.2 us  [the longest x1 10 us: gather(): gathered = lax.all_to_all(whole, 'z', 0, 0, tiled=True)]
  transfers between devices with their start and end apart: 4 -> 4, of which waited for: 3 -> 2; matrix products, arithmetic and copies ran while one was open for 0% -> 0% of each run, Pallas kernels for 1% -> 6%
where the time goes in v2:
time: 111 us; the launch traced here: 110 us
  blocking collectives  64.6 us (58%)
  starting transfers between devices  21.2 us (19%)
  Pallas kernels  12.4 us (11%)
  waiting for transfers between devices  11.2 us (10%)
    all_to_all x3, blocking collectives, exchange(): return lax.all_to_all(x, ('x', 'c', 'y'), 0, 0, tiled=True)  55.5 us
    pallas_call x12, Pallas kernels, run(): pl.pallas_call(body, out_shape=[a if n in keep else pltpu.VMEM(a.shape, a...  12.4 us
    all_to_all x1, starting transfers between devices, gather(): gathered = lax.all_to_all(whole, 'z', 0, 0, tiled=True)  10 us
    all_to_all x1, blocking collectives, gather(): gathered = lax.all_to_all(whole, 'z', 0, 0, tiled=True)  9.15 us
    all_to_all x1, starting transfers between devices, exchange(): return lax.all_to_all(x, ('x', 'c', 'y'), 0, 0, tiled=True)  7.12 us
    all_to_all x1, waiting for transfers between devices, gather(): gathered = lax.all_to_all(whole, 'z', 0, 0, tiled=True)  5.87 us
    ppermute x1, waiting for transfers between devices, shards(): below = lax.ppermute(edge_rows(v_late, g_late, 0), 'y', downward)  5.28 us
    ppermute x1, starting transfers between devices, above_and_terms(): above = lax.ppermute(edge_rows(v, g, rows - 1), 'y', upward)  2.73 us
  transfers between devices with their start and end apart: 4, of which 2 were waited for; matrix products, arithmetic and copies ran while one was open for 0% of the time, Pallas kernels for 6%

profile of v2, /device:TPU:1, one launch (start us, length us, event | category | flops | bytes accessed | tf_op | source)
XLA Modules:
  0.0 110.1 jit_solution(989932114231386996)
XLA Ops:
  0.6 0.0 copy-start
  0.6 0.0 copy-start.1
  0.7 1.7 %state.1 = f32[320,128]{1,0:T(8,128)S(1)} custom-call(bf16[5,26,1120]{2,1,0:T(8,128)(2,1)} %bitcast.28, bf16[5,26,1120]{2,1,0:T(8,128)(2,1)} %bitcast.18), custom_call_target="tpu_custom_call" | custom-call | tf_op jit(solution)/shard_map/state/pallas_call | solution.py:311
  2.3 21.8 %all_to_all.30.received = f32[64,1,640]{2,1,0:T(1,128)S(1)} all-to-all(f32[64,1,640]{2,1,0:T(1,128)S(1)} %bitcast.32), channel_id=1, replica_groups=mesh['z'=8,'x'=4,'c'=2,'y'=8] {'x','c','y'}, dimensions={0} | all-to-all | bytes 327680 | tf_op jit(solution)/shard_map/all_to_all | solution.py:344
  24.1 0.0 copy-done
  24.1 0.0 copy-done.1
  24.1 2.7 %collective-permute-start = (bf16[2,26,1120]{2,1,0:T(8,128)(2,1)S(1)}, bf16[2,26,1120]{2,1,0:T(8,128)(2,1)S(1)}, u32[]{:S(2)}, u32[]{:S(2)}) collective-permute-start(bf16[2,26,1120]{2,1,0:T(8,128)(2,1)S(1)} %edge.2), channel_id=1, source_target_pairs={{0,1},{1,2},{2,3},{3,4},{4,5},{5,6},{6,7},{8,9},{9,10},{10,11},{11... | collective-permute-start | bytes 349448 | tf_op jit(solution)/shard_map/ppermute | solution.py:374
  26.9 0.6 totals.2
  27.5 10.0 %all-to-all-start.1 = ((f32[8,1,640]{2,1,0:T(1,128)}), f32[8,1,640]{2,1,0:T(1,128)S(1)}, u32[]{:S(2)}, u32[]{:S(2)}) async-start(f32[8,1,640]{2,1,0:T(1,128)} %get-tuple-element.29), calls=%async_computation.1 | async-start | bytes 40960 | tf_op jit(solution)/shard_map/all_to_all | solution.py:355
  37.5 0.0 collective-permute-done.above
  37.6 0.8 terms.1
  38.3 0.0 copy-start.2
  38.3 5.9 %all-to-all-done.1.received = f32[8,1,640]{2,1,0:T(1,128)S(1)} async-done(((f32[8,1,640]{2,1,0:T(1,128)}), f32[8,1,640]{2,1,0:T(1,128)S(1)}, u32[]{:S(2)}, u32[]{:S(2)}) %all-to-all-start.1) | async-done | bytes 20512 | tf_op jit(solution)/shard_map/all_to_all | solution.py:355
  44.2 17.5 %all_to_all.31 = f32[64,1,640]{2,1,0:T(1,128)S(1)} all-to-all(f32[64,1,640]{2,1,0:T(1,128)S(1)} %prefix.1), channel_id=1, replica_groups=mesh['z'=8,'x'=4,'c'=2,'y'=8] {'x','c','y'}, dimensions={0} | all-to-all | bytes 327680 | tf_op jit(solution)/shard_map/all_to_all | solution.py:344
  61.7 0.0 copy-done.2
  61.7 2.0 %query.1 = f32[384,128]{1,0:T(8,128)S(1)} custom-call(bf16[5,26,1120]{2,1,0:T(8,128)(2,1)S(1)} %bitcast.26, bf16[5,26,1120]{2,1,0:T(8,128)(2,1)S(1)} %bitcast.14, f32[320,128]{1,0:T(8,128)S(1)} %bitcast.24, f32[16,1152]{1,0:T(8,128)S(1)} %terms.1), custom_call_target="tpu_custom_call" | custom-call | tf_op jit(solution)/shard_map/query/pallas_call | solution.py:311
  63.7 16.2 %all_to_all.32.received = f32[64,1,768]{2,1,0:T(1,128)S(1)} all-to-all(f32[64,1,768]{2,1,0:T(1,128)S(1)} %bitcast.31), channel_id=1, replica_groups=mesh['z'=8,'x'=4,'c'=2,'y'=8] {'x','c','y'}, dimensions={0} | all-to-all | bytes 393216 | tf_op jit(solution)/shard_map/all_to_all | solution.py:344
  79.9 9.1 %all_to_all.33.received = f32[8,1,768]{2,1,0:T(1,128)S(1)} all-to-all(f32[8,1,768]{2,1,0:T(1,128)S(1)} %get-tuple-element.36), channel_id=1, replica_groups=mesh['z'=8,'x'=4,'c'=2,'y'=8] {'z'}, dimensions={0} | all-to-all | bytes 49152 | tf_op jit(solution)/shard_map/all_to_all | solution.py:355
  89.1 0.7 suffix.1
  89.8 7.1 %all-to-all-start.5 = ((f32[64,1,768]{2,1,0:T(1,128)}), f32[64,1,768]{2,1,0:T(1,128)S(1)}, u32[]{:S(2)}, u32[]{:S(2)}) async-start(f32[64,1,768]{2,1,0:T(1,128)} %suffix.1), calls=%async_computation.5 | async-start | bytes 393216 | tf_op jit(solution)/shard_map/all_to_all | solution.py:344
  97.0 0.0 copy-start.4
  97.0 1.3 %collective-permute-start.1 = (bf16[2,26,1120]{2,1,0:T(8,128)(2,1)S(1)}, bf16[2,26,1120]{2,1,0:T(8,128)(2,1)S(1)}, u32[]{:S(2)}, u32[]{:S(2)}) collective-permute-start(bf16[2,26,1120]{2,1,0:T(8,128)(2,1)S(1)} %edge.3), channel_id=1, source_target_pairs={{1,0},{2,1},{3,2},{4,3},{5,4},{6,5},{7,6},{9,8},{10,9},{11,10},{12... | collective-permute-start | bytes 349448 | tf_op jit(solution)/shard_map/ppermute | solution.py:388
  98.3 0.0 copy-done.4
  98.3 2.7 %grad.1 = (bf16[5,26,1120]{2,1,0:T(8,128)(2,1)}, f32[5,32,1152]{2,1,0:T(8,128)S(1)}) custom-call(bf16[5,26,1120]{2,1,0:T(8,128)(2,1)S(1)} %bitcast.27, bf16[5,26,1120]{2,1,0:T(8,128)(2,1)S(1)} %bitcast.16, f32[320,128]{1,0:T(8,128)S(1)} %bitcast.25), custom_call_target="tpu_custom_call" | custom-call | tf_op jit(solution)/shard_map/grad/pallas_call | solution.py:311
  101.1 5.3 %collective-permute-done.1.below = bf16[2,26,1120]{2,1,0:T(8,128)(2,1)S(1)} collective-permute-done((bf16[2,26,1120]{2,1,0:T(8,128)(2,1)S(1)}, bf16[2,26,1120]{2,1,0:T(8,128)(2,1)S(1)}, u32[]{:S(2)}, u32[]{:S(2)}) %collective-permute-start.1) | collective-permute-done | bytes 116512 | tf_op jit(solution)/shard_map/ppermute | solution.py:388
  106.3 0.0 copy-start.3
  106.3 2.1 %mixed.1 = (bf16[5,26,1120]{2,1,0:T(8,128)(2,1)}, f32[5,32,1152]{2,1,0:T(8,128)S(1)}) custom-call(bf16[5,26,1120]{2,1,0:T(8,128)(2,1)S(1)} %bitcast.22, bf16[5,26,1120]{2,1,0:T(8,128)(2,1)S(1)} %bitcast.17, bf16[2,26,1120]{2,1,0:T(8,128)(2,1)S(1)} %collective-permute-done.above, bf16[2,26,1120]{2,1,0:T(8,128)(2,1)S(1)} %collective-permute-done.1.below, ...), custom_call_target="tpu_custom_call" | custom-call | tf_op jit(solution)/shard_map/mixed/pallas_call | solution.py:311
  108.5 0.0 all-to-all-done.5
  108.5 0.0 copy-done.3
  108.5 1.6 %key.1 = (bf16[5,26,1120]{2,1,0:T(8,128)(2,1)}, bf16[5,26,1120]{2,1,0:T(8,128)(2,1)}, f32[3,3,1120]{2,1,0:T(4,128)}) custom-call(bf16[5,26,1120]{2,1,0:T(8,128)(2,1)S(1)} %bitcast.29, bf16[5,26,1120]{2,1,0:T(8,128)(2,1)S(1)} %bitcast.23, f32[384,128]{1,0:T(8,128)S(1)} %bitcast.30, f32[5,32,1152]{2,1,0:T(8,128)S(1)} %get-tuple-element.47.refs_3_), custom_call_target="tpu_custom_call" | custom-call | tf_op jit(solution)/shard_map/key/pallas_call | solution.py:311
  (5 shorter events, 0.1 us)
Async XLA Ops:
  0.6 23.5 %copy-start = (bf16[1,5,26,1120]{3,2,1,0:T(8,128)(2,1)S(1)}, bf16[1,5,26,1120]{3,2,1,0:T(8,128)(2,1)}, u32[]{:S(2)}) copy-start(bf16[1,5,26,1120]{3,2,1,0:T(8,128)(2,1)} %param.8) | copy-start | bytes 873604
  0.6 23.5 %copy-start.1 = (bf16[1,5,26,1120]{3,2,1,0:T(8,128)(2,1)S(1)}, bf16[1,5,26,1120]{3,2,1,0:T(8,128)(2,1)}, u32[]{:S(2)}) copy-start(bf16[1,5,26,1120]{3,2,1,0:T(8,128)(2,1)} %param.7) | copy-start | bytes 873604
  24.1 13.4 %collective-permute-start = (bf16[2,26,1120]{2,1,0:T(8,128)(2,1)S(1)}, bf16[2,26,1120]{2,1,0:T(8,128)(2,1)S(1)}, u32[]{:S(2)}, u32[]{:S(2)}) collective-permute-start(bf16[2,26,1120]{2,1,0:T(8,128)(2,1)S(1)} %edge.2), channel_id=1, source_target_pairs={{0,1},{1,2},{2,3},{3,4},{4,5},{5,6},{6,7},{8,9},{9,10},{10,11},{11... | collective-permute-start | bytes 349448 | tf_op jit(solution)/shard_map/ppermute | solution.py:374
  27.5 16.7 %all-to-all-start.1 = ((f32[8,1,640]{2,1,0:T(1,128)}), f32[8,1,640]{2,1,0:T(1,128)S(1)}, u32[]{:S(2)}, u32[]{:S(2)}) async-start(f32[8,1,640]{2,1,0:T(1,128)} %get-tuple-element.29), calls=%async_computation.1 | async-start | bytes 40960 | tf_op jit(solution)/shard_map/all_to_all | solution.py:355
  38.3 23.4 %copy-start.2 = (bf16[1,5,26,1120]{3,2,1,0:T(8,128)(2,1)S(1)}, bf16[1,5,26,1120]{3,2,1,0:T(8,128)(2,1)}, u32[]{:S(2)}) copy-start(bf16[1,5,26,1120]{3,2,1,0:T(8,128)(2,1)} %param.5) | copy-start | bytes 873604
  89.8 18.6 %all-to-all-start.5 = ((f32[64,1,768]{2,1,0:T(1,128)}), f32[64,1,768]{2,1,0:T(1,128)S(1)}, u32[]{:S(2)}, u32[]{:S(2)}) async-start(f32[64,1,768]{2,1,0:T(1,128)} %suffix.1), calls=%async_computation.5 | async-start | bytes 393216 | tf_op jit(solution)/shard_map/all_to_all | solution.py:344
  97.0 1.3 %copy-start.4 = (f32[3,3,1120]{2,1,0:T(4,128)S(1)}, f32[3,3,1120]{2,1,0:T(4,128)}, u32[]{:S(2)}) copy-start(f32[3,3,1120]{2,1,0:T(4,128)} %param.9) | copy-start | bytes 120964
  97.0 9.3 %collective-permute-start.1 = (bf16[2,26,1120]{2,1,0:T(8,128)(2,1)S(1)}, bf16[2,26,1120]{2,1,0:T(8,128)(2,1)S(1)}, u32[]{:S(2)}, u32[]{:S(2)}) collective-permute-start(bf16[2,26,1120]{2,1,0:T(8,128)(2,1)S(1)} %edge.3), channel_id=1, source_target_pairs={{1,0},{2,1},{3,2},{4,3},{5,4},{6,5},{7,6},{9,8},{10,9},{11,10},{12... | collective-permute-start | bytes 349448 | tf_op jit(solution)/shard_map/ppermute | solution.py:388
  106.3 2.1 %copy-start.3 = (bf16[1,5,26,1120]{3,2,1,0:T(8,128)(2,1)S(1)}, bf16[1,5,26,1120]{3,2,1,0:T(8,128)(2,1)}, u32[]{:S(2)}) copy-start(bf16[1,5,26,1120]{3,2,1,0:T(8,128)(2,1)} %param.6) | copy-start | bytes 873604

commit v3 on v2

--- a/solution.py
+++ b/solution.py
@@ -14,6 +14,7 @@
 WIDTH = HEADS * HEAD_DIM
 GROUPS = -(-WIDTH // LANES)
 PAD = 32
+BATCH = 3
 STATE_ROWS = GROUPS * HEAD_DIM
 TAIL_ROW = STATE_ROWS + 8 * GROUPS
 
@@ -38,9 +39,13 @@
     return lax.dot_general(a, b, (((0,), (0,)), ((), ())), preferred_element_type=f32)
 
 
-def split(x):
+def split(x, axis):
     high = x.astype(bf16)
-    return high, (x - high.astype(f32)).astype(bf16)
+    return jnp.concatenate([high, (x - high.astype(f32)).astype(bf16)], axis=axis)
+
+
+def twice(x):
+    return jnp.concatenate([x, x], axis=1)
 
 
 def same_head():
@@ -86,15 +91,21 @@
     )
 
 
+def batches():
+    return [range(n, min(n + BATCH, GROUPS)) for n in range(0, GROUPS, BATCH)]
+
+
 def fill_rows(scratch, ref, rows):
     scratch[...] = jnp.zeros_like(scratch)
     for r in range(rows):
         scratch[r, pl.ds(0, ref.shape[1]), pl.ds(0, WIDTH)] = ref[r]
 
 
-def edge_kernel(row, v_ref, g_ref, out):
+def edge_kernel(v_ref, g_ref, first, last):
+    rows = v_ref.shape[0]
     for n, ref in enumerate((v_ref, g_ref)):
-        out[n] = ref[row]
+        first[n] = ref[0]
+        last[n] = ref[rows - 1]
 
 
 def state_kernel(k_ref, v_ref, send, k_s, v_s):
@@ -104,14 +115,16 @@
     clear_extra(send)
     heads = lane_head()
     token = lax.broadcasted_iota(jnp.int32, (rows, PAD, LANES), 1) < columns
-    for group in range(GROUPS):
-        lanes = pl.ds(group * LANES, LANES)
-        k_raw = k_s[:, :, lanes].astype(f32)
-        feat = jnp.where(k_raw > 0, k_raw + 1.0, jnp.exp(jnp.minimum(k_raw, 0.0)))
-        feat = jnp.where(token, feat, 0.0).astype(bf16).reshape(rows * PAD, LANES)
-        value = v_s[:, :, lanes].reshape(rows * PAD, LANES)
-        send[state_rows(group), :] = compact(dot_tn(feat, value), heads)
-        send[norm_row(group), :] = jnp.sum(feat.astype(f32), axis=0, keepdims=True)
+    for groups in batches():
+        at = [pl.ds(group * LANES, LANES) for group in groups]
+        raw = [k_s[:, :, lanes].astype(f32) for lanes in at]
+        feat = [jnp.where(x > 0, x + 1.0, jnp.exp(jnp.minimum(x, 0.0))) for x in raw]
+        feat = [jnp.where(token, x, 0.0).astype(bf16).reshape(rows * PAD, LANES) for x in feat]
+        value = [v_s[:, :, lanes].reshape(rows * PAD, LANES) for lanes in at]
+        whole = [dot_tn(x, y) for x, y in zip(feat, value)]
+        for group, x, product in zip(groups, feat, whole):
+            send[norm_row(group), :] = jnp.sum(x.astype(f32), axis=0, keepdims=True)
+            send[state_rows(group), :] = compact(product, heads)
 
 
 def totals_kernel(received, frames, send):
@@ -197,24 +210,23 @@
             terms[pl.ds(1 + n, 1), lanes] = jnp.sum(term, axis=0, keepdims=True)
 
 
-def attend(q_s, g_s, received, group, same, ones):
+def attend(q_s, g_s, received, groups, same, ones):
     tokens = q_s.shape[0] * PAD
-    wide = span(group)[1]
-    lanes = pl.ds(group * LANES, LANES)
-    q_raw = q_s[:, :, lanes].reshape(tokens, LANES).astype(f32)
-    low = jnp.exp(jnp.minimum(q_raw, 0.0))
-    feat = jnp.where(q_raw > 0, q_raw + 1.0, low).astype(bf16)
-    slope = jnp.where(q_raw > 0, 1.0, low)
-    grad = g_s[:, :, lanes].reshape(tokens, LANES)
-    state = split(expand(received[state_rows(group), :], same))
-    norm = received[norm_row(group), :]
-    norm = jnp.where(lax.broadcasted_iota(jnp.int32, (1, LANES), 1) < wide, norm, 1.0)
-    num = dot(feat, state[0]) + dot(feat, state[1])
-    a, b = split(feat.astype(f32) * norm)
-    inverse = 1.0 / (dot(a, ones) + dot(b, ones))
-    a, b = split(grad.astype(f32) * num)
-    along = (dot(a, ones) + dot(b, ones)) * inverse
-    return feat, slope, grad, state, norm, num, inverse, along
+    lane = lax.broadcasted_iota(jnp.int32, (1, LANES), 1)
+    at = [pl.ds(group * LANES, LANES) for group in groups]
+    raw = [q_s[:, :, lanes].reshape(tokens, LANES).astype(f32) for lanes in at]
+    low = [jnp.exp(jnp.minimum(x, 0.0)) for x in raw]
+    feat = [jnp.where(x > 0, x + 1.0, y).astype(bf16) for x, y in zip(raw, low)]
+    slope = [jnp.where(x > 0, 1.0, y) for x, y in zip(raw, low)]
+    grad = [g_s[:, :, lanes].reshape(tokens, LANES) for lanes in at]
+    state = [expand(received[state_rows(group), :], same) for group in groups]
+    norm = [jnp.where(lane < span(n)[1], received[norm_row(n), :], 1.0) for n in groups]
+    den = [dot(split(x.astype(f32) * y, 1), ones) for x, y in zip(feat, norm)]
+    num = [dot(twice(x), split(y, 0)) for x, y in zip(feat, state)]
+    inverse = [1.0 / x for x in den]
+    along = [dot(split(x.astype(f32) * y, 1), ones) for x, y in zip(grad, num)]
+    along = [x * y for x, y in zip(along, inverse)]
+    return list(zip(groups, feat, slope, grad, state, norm, num, inverse, along))
 
 
 def query_kernel(q_ref, g_ref, received, terms, send, q_s, g_s):
@@ -224,15 +236,18 @@
     clear_extra(send)
     heads, same = lane_head(), same_head()
     ones = same.astype(f32).astype(bf16)
-    for group in range(GROUPS):
-        feat, _, grad, _, _, _, inverse, along = attend(q_s, g_s, received, group, same, ones)
-        scaled = feat.astype(f32) * inverse
-        a, b = split(scaled)
-        send[state_rows(group), :] = compact(dot_tn(grad, a) + dot_tn(grad, b), heads)
-        lanes = pl.ds(group * LANES, LANES)
-        send[head_rows(group, 8), :] = terms[pl.ds(0, 8), lanes]
-        send[head_rows(group, 1), :] = -jnp.sum(scaled * along, axis=0, keepdims=True)
-        send[tail_rows(group), :] = terms[pl.ds(8, 2), lanes]
+    ones = jnp.concatenate([ones, ones], axis=0)
+    for groups in batches():
+        parts = attend(q_s, g_s, received, groups, same, ones)
+        scaled = [part[1].astype(f32) * part[7] for part in parts]
+        pairs = [dot_tn(part[3], split(x, 1)) for part, x in zip(parts, scaled)]
+        for part, x, pair in zip(parts, scaled, pairs):
+            group, along = part[0], part[8]
+            send[state_rows(group), :] = compact(pair[:, :LANES] + pair[:, LANES:], heads)
+            lanes = pl.ds(group * LANES, LANES)
+            send[head_rows(group, 8), :] = terms[pl.ds(0, 8), lanes]
+            send[head_rows(group, 1), :] = -jnp.sum(x * along, axis=0, keepdims=True)
+            send[tail_rows(group), :] = terms[pl.ds(8, 2), lanes]
 
 
 def grad_kernel(q_ref, g_ref, received, q_grad, attn, q_s, g_s):
@@ -241,15 +256,16 @@
     fill_rows(g_s, g_ref, rows)
     same = same_head()
     ones = same.astype(f32).astype(bf16)
-    for group in range(GROUPS):
-        start, wide = span(group)
-        _, slope, grad, state, norm, num, inverse, along = attend(
-            q_s, g_s, received, group, same, ones
-        )
-        back = dot_nt(grad, state[0]) + dot_nt(grad, state[1])
-        back = ((back - along * norm) * inverse * slope).reshape(rows, PAD, LANES)
-        q_grad[:, :, pl.ds(start, wide)] = back[:, :columns, :wide].astype(bf16)
-        attn[:, :, pl.ds(start, LANES)] = (num * inverse).reshape(rows, PAD, LANES)
+    ones = jnp.concatenate([ones, ones], axis=0)
+    for groups in batches():
+        for group, _, slope, grad, state, norm, num, inverse, along in attend(
+            q_s, g_s, received, groups, same, ones
+        ):
+            start, wide = span(group)
+            back = dot_nt(twice(grad), split(state, 1))
+            back = ((back - along * norm) * inverse * slope).reshape(rows, PAD, LANES)
+            q_grad[:, :, pl.ds(start, wide)] = back[:, :columns, :wide].astype(bf16)
+            attn[:, :, pl.ds(start, LANES)] = (num * inverse).reshape(rows, PAD, LANES)
 
 
 def mixed_kernel(v_ref, g_ref, above, below, w_ref, attn, mixed, v_local, v_s, g_s):
@@ -280,26 +296,26 @@
     fill_rows(k_s, k_ref, rows)
     fill_rows(v_s, v_ref, rows)
     same = same_head()
-    for group in range(GROUPS):
-        start, wide = span(group)
-        lanes = pl.ds(start, LANES)
-        k_raw = k_s[:, :, lanes].reshape(tokens, LANES).astype(f32)
-        low = jnp.exp(jnp.minimum(k_raw, 0.0))
-        feat = jnp.where(k_raw > 0, k_raw + 1.0, low).astype(bf16)
-        slope = jnp.where(k_raw > 0, 1.0, low)
-        value = v_s[:, :, lanes].reshape(tokens, LANES)
-        high, rest = split(expand(received[state_rows(group), :], same))
-        ahead = received[head_rows(group), :]
-        back = dot(value, high) + dot(value, rest) + ahead[0:1]
-        back = (back * slope).reshape(rows, PAD, LANES)
-        k_grad[:, :, pl.ds(start, wide)] = back[:, :columns, :wide].astype(bf16)
-        here = (dot_nt(feat, high) + dot_nt(feat, rest)).reshape(rows, PAD, LANES)
-        here = here + v_local[:, :, lanes]
-        v_grad[:, :, pl.ds(start, wide)] = here[:, :columns, :wide].astype(bf16)
-        tail = received[tail_rows(group), :]
-        for n in range(9):
-            term = ahead[n + 1 : n + 2] if n < 7 else tail[n - 7 : n - 6]
-            kernel_grad[n // 3, pl.ds(n % 3, 1), pl.ds(start, wide)] = (term * scale)[:, :wide]
+    for groups in batches():
+        at = [pl.ds(group * LANES, LANES) for group in groups]
+        state = [expand(received[state_rows(group), :], same) for group in groups]
+        value = [v_s[:, :, lanes].reshape(tokens, LANES) for lanes in at]
+        back = [dot(twice(x), split(y, 0)) for x, y in zip(value, state)]
+        raw = [k_s[:, :, lanes].reshape(tokens, LANES).astype(f32) for lanes in at]
+        low = [jnp.exp(jnp.minimum(x, 0.0)) for x in raw]
+        feat = [jnp.where(x > 0, x + 1.0, y).astype(bf16) for x, y in zip(raw, low)]
+        slope = [jnp.where(x > 0, 1.0, y) for x, y in zip(raw, low)]
+        forth = [dot_nt(twice(x), split(y, 1)) for x, y in zip(feat, state)]
+        for n, group in enumerate(groups):
+            start, wide = span(group)
+            ahead, tail = received[head_rows(group), :], received[tail_rows(group), :]
+            grad = ((back[n] + ahead[0:1]) * slope[n]).reshape(rows, PAD, LANES)
+            k_grad[:, :, pl.ds(start, wide)] = grad[:, :columns, :wide].astype(bf16)
+            grad = forth[n].reshape(rows, PAD, LANES) + v_local[:, :, at[n]]
+            v_grad[:, :, pl.ds(start, wide)] = grad[:, :columns, :wide].astype(bf16)
+            for m in range(9):
+                term = ahead[m + 1 : m + 2] if m < 7 else tail[m - 7 : m - 6]
+                kernel_grad[m // 3, pl.ds(m % 3, 1), pl.ds(start, wide)] = (term * scale)[:, :wide]
 
 
 def call(body, out_shape, name, scratch=(), plain=(), keep=()):
@@ -346,46 +362,36 @@
     def scatter(send):
         return exchange(send.reshape(peers, 1, -1))
 
-    def gather(received, body, name, beside, then):
-        received, v_now, g_now = lax.optimization_barrier((received, v, g))
+    def gather(received, body, name, then):
         piece = received.shape[1:]
         sums, whole = call(
             totals_kernel, (shape((frames, *piece), f32), shape((planes, *piece), f32)), "totals"
         )(received)
         gathered = lax.all_to_all(whole, "z", 0, 0, tiled=True)
-        done = beside(v_now, g_now)
-        gathered, done, then = lax.optimization_barrier((gathered, done, then))
+        gathered, then = lax.optimization_barrier((gathered, then))
         (back,) = call(body, (shape(received.shape, f32),), name)(gathered, sums)
-        return exchange(back).reshape(-1, LANES), done, then
-
-    def edge_rows(v, g, row):
-        def body(*refs):
-            edge_kernel(row, *refs)
-
-        return call(body, (edge_shape,), "edge")(v, g)[0]
+        return exchange(back).reshape(-1, LANES), then
 
     ends = lax.axis_size("y") - 1
     upward = [(i, i + 1) for i in range(ends)]
     downward = [(i + 1, i) for i in range(ends)]
+    first, last = call(edge_kernel, (edge_shape,) * 2, "edges")(v, g)
+    above = lax.ppermute(last, "y", upward)
+    below = lax.ppermute(first, "y", downward)
     (send,) = call(
         state_kernel, (flat(STATE_ROWS + GROUPS),), "state", [token_scratch] * 2, plain=(0, 1)
     )(k, v)
-    def above_and_terms(v, g):
-        above = lax.ppermute(edge_rows(v, g, rows - 1), "y", upward)
-        return above, *call(terms_kernel, (shape((16, lanes), f32),), "terms", [row_scratch] * 2)(
-            v, g, above
-        )
-
-    state, (above, terms), _ = gather(
-        scatter(send), prefix_kernel, "prefix", above_and_terms, ()
+    received = scatter(send)
+    (terms,) = call(terms_kernel, (shape((16, lanes), f32),), "terms", [row_scratch] * 2)(
+        v, g, above
     )
+    state, (terms, below) = gather(received, prefix_kernel, "prefix", (terms, below))
     (send,) = call(
         query_kernel, (flat(STATE_ROWS + 10 * GROUPS),), "query", [token_scratch] * 2
     )(q, g, state, terms)
-    later, _, (q_late, v_late, g_late, state) = gather(
-        scatter(send), suffix_kernel, "suffix", lambda v, g: (), (q, v, g, state)
+    later, (q_late, v_late, g_late, state) = gather(
+        scatter(send), suffix_kernel, "suffix", (q, v, g, state)
     )
-    below = lax.ppermute(edge_rows(v_late, g_late, 0), "y", downward)
     weight = jnp.pad(local_kernel_weight, ((0, 0), (0, 0), (0, lanes - width)))
     q_grad, attn = call(grad_kernel, (tokens, padded), "grad", [token_scratch] * 2, keep=(0,))(
         q_late, g_late, state

time: 111 us -> 108 us (0.973)
  blocking collectives: 64.6 us -> 44 us
  starting transfers between devices: 21.2 us -> 33.5 us
  waiting for transfers between devices: 11.2 us -> 18.2 us
    all_to_all x3 -> x2, blocking collectives: 55.5 us -> 34.8 us  [exchange(): return lax.all_to_all(x, ('x', 'c', 'y'), 0, 0, tiled=True)]
    all_to_all x1 -> x2, waiting for transfers between devices: 0.01 us -> 12.3 us  [exchange(): return lax.all_to_all(x, ('x', 'c', 'y'), 0, 0, tiled=True)]
    all_to_all x1 -> x2, starting transfers between devices: 7.12 us -> 18.9 us  [exchange(): return lax.all_to_all(x, ('x', 'c', 'y'), 0, 0, tiled=True)]
    ppermute x2, waiting for transfers between devices: 5.28 us -> 0.01 us  [the longest x1 0.01 us: shards(): below = lax.ppermute(first, 'y', downward)]
    pallas_call x12 -> x11, Pallas kernels: 12.4 us -> 11.5 us  [run(): pl.pallas_call(body, out_shape=[a if n in keep else pltpu.VMEM(a.shape, a...]
  transfers between devices with their start and end apart: 4 -> 5, of which waited for: 2 -> 3; matrix products, arithmetic and copies ran while one was open for 0% -> 0% of each run, Pallas kernels for 6% -> 5%
where the time goes in v3:
time: 108 us
  blocking collectives  44 us (41%)
  starting transfers between devices  33.5 us (31%)
  waiting for transfers between devices  18.2 us (17%)
  Pallas kernels  11.5 us (11%)
    all_to_all x2, blocking collectives, exchange(): return lax.all_to_all(x, ('x', 'c', 'y'), 0, 0, tiled=True)  34.8 us
    all_to_all x2, starting transfers between devices, exchange(): return lax.all_to_all(x, ('x', 'c', 'y'), 0, 0, tiled=True)  18.9 us
    all_to_all x2, waiting for transfers between devices, exchange(): return lax.all_to_all(x, ('x', 'c', 'y'), 0, 0, tiled=True)  12.3 us
    pallas_call x11, Pallas kernels, run(): pl.pallas_call(body, out_shape=[a if n in keep else pltpu.VMEM(a.shape, a...  11.5 us
    all_to_all x1, starting transfers between devices, gather(): gathered = lax.all_to_all(whole, 'z', 0, 0, tiled=True)  10 us
    all_to_all x1, blocking collectives, gather(): gathered = lax.all_to_all(whole, 'z', 0, 0, tiled=True)  9.15 us
    all_to_all x1, waiting for transfers between devices, gather(): gathered = lax.all_to_all(whole, 'z', 0, 0, tiled=True)  5.86 us
    ppermute x1, starting transfers between devices, shards(): above = lax.ppermute(last, 'y', upward)  3.29 us
  transfers between devices with their start and end apart: 5, of which 3 were waited for; matrix products, arithmetic and copies ran while one was open for 0% of the time, Pallas kernels for 5%

profile of v3, /device:TPU:1, one launch (start us, length us, event | category | flops | bytes accessed | tf_op | source)
XLA Modules:
  0.0 107.9 jit_solution(9936351212445956291)
XLA Ops:
  0.6 0.0 copy-start
  0.6 0.0 copy-start.1
  0.7 2.4 %state.1 = f32[320,128]{1,0:T(8,128)} custom-call(bf16[5,26,1120]{2,1,0:T(8,128)(2,1)} %bitcast.26, bf16[5,26,1120]{2,1,0:T(8,128)(2,1)} %bitcast.17), custom_call_target="tpu_custom_call" | custom-call | tf_op jit(solution)/shard_map/state/pallas_call | solution.py:327
  3.0 11.6 %all-to-all-start = ((f32[64,1,640]{2,1,0:T(1,128)}), f32[64,1,640]{2,1,0:T(1,128)S(1)}, u32[]{:S(2)}, u32[]{:S(2)}) async-start(f32[64,1,640]{2,1,0:T(1,128)} %bitcast.4), calls=%async_computation | async-start | bytes 327680 | tf_op jit(solution)/shard_map/all_to_all | solution.py:360
  14.6 0.0 copy-done
  14.7 0.0 copy-done.1
  14.7 3.3 %collective-permute-start = (bf16[2,26,1120]{2,1,0:T(8,128)(2,1)S(1)}, bf16[2,26,1120]{2,1,0:T(8,128)(2,1)S(1)}, u32[]{:S(2)}, u32[]{:S(2)}) collective-permute-start(bf16[2,26,1120]{2,1,0:T(8,128)(2,1)S(1)} %get-tuple-element.27), channel_id=1, source_target_pairs={{0,1},{1,2},{2,3},{3,4},{4,5},{5,6},{6,7},{8,9},{9,10},{10,11},{11... | collective-permute-start | bytes 349448 | tf_op jit(solution)/shard_map/ppermute | solution.py:379
  18.0 1.3 %collective-permute-start.1 = (bf16[2,26,1120]{2,1,0:T(8,128)(2,1)S(1)}, bf16[2,26,1120]{2,1,0:T(8,128)(2,1)S(1)}, u32[]{:S(2)}, u32[]{:S(2)}) collective-permute-start(bf16[2,26,1120]{2,1,0:T(8,128)(2,1)S(1)} %get-tuple-element.28), channel_id=1, source_target_pairs={{1,0},{2,1},{3,2},{4,3},{5,4},{6,5},{7,6},{9,8},{10,9},{11,10},{12... | collective-permute-start | bytes 349448 | tf_op jit(solution)/shard_map/ppermute | solution.py:380
  19.3 5.7 %all-to-all-done.received = f32[64,1,640]{2,1,0:T(1,128)S(1)} async-done(((f32[64,1,640]{2,1,0:T(1,128)}), f32[64,1,640]{2,1,0:T(1,128)S(1)}, u32[]{:S(2)}, u32[]{:S(2)}) %all-to-all-start) | async-done | bytes 163872 | tf_op jit(solution)/shard_map/all_to_all | solution.py:360
  25.0 0.6 totals.2
  25.6 10.0 %all-to-all-start.1 = ((f32[8,1,640]{2,1,0:T(1,128)}), f32[8,1,640]{2,1,0:T(1,128)S(1)}, u32[]{:S(2)}, u32[]{:S(2)}) async-start(f32[8,1,640]{2,1,0:T(1,128)} %get-tuple-element.26), calls=%async_computation.1 | async-start | bytes 40960 | tf_op jit(solution)/shard_map/all_to_all | solution.py:370
  35.7 0.0 collective-permute-done.above
  35.7 0.8 terms.1
  36.4 0.0 copy-start.2
  36.4 0.0 collective-permute-done.1.below
  36.4 5.9 %all-to-all-done.1.received = f32[8,1,640]{2,1,0:T(1,128)S(1)} async-done(((f32[8,1,640]{2,1,0:T(1,128)}), f32[8,1,640]{2,1,0:T(1,128)S(1)}, u32[]{:S(2)}, u32[]{:S(2)}) %all-to-all-start.1) | async-done | bytes 20512 | tf_op jit(solution)/shard_map/all_to_all | solution.py:370
  42.3 18.7 %all_to_all.30 = f32[64,1,640]{2,1,0:T(1,128)S(1)} all-to-all(f32[64,1,640]{2,1,0:T(1,128)S(1)} %prefix.1), channel_id=1, replica_groups=mesh['z'=8,'x'=4,'c'=2,'y'=8] {'x','c','y'}, dimensions={0} | all-to-all | bytes 327680 | tf_op jit(solution)/shard_map/all_to_all | solution.py:360
  61.0 0.0 copy-done.2
  61.0 1.3 %query.1 = f32[384,128]{1,0:T(8,128)S(1)} custom-call(bf16[5,26,1120]{2,1,0:T(8,128)(2,1)S(1)} %bitcast.24, bf16[5,26,1120]{2,1,0:T(8,128)(2,1)S(1)} %bitcast.14, f32[320,128]{1,0:T(8,128)S(1)} %bitcast.22, f32[16,1152]{1,0:T(8,128)S(1)} %terms.1), custom_call_target="tpu_custom_call" | custom-call | tf_op jit(solution)/shard_map/query/pallas_call | solution.py:327
  62.3 16.2 %all_to_all.31.received = f32[64,1,768]{2,1,0:T(1,128)S(1)} all-to-all(f32[64,1,768]{2,1,0:T(1,128)S(1)} %bitcast.29), channel_id=1, replica_groups=mesh['z'=8,'x'=4,'c'=2,'y'=8] {'x','c','y'}, dimensions={0} | all-to-all | bytes 393216 | tf_op jit(solution)/shard_map/all_to_all | solution.py:360
  78.5 9.1 %all_to_all.32.received = f32[8,1,768]{2,1,0:T(1,128)S(1)} all-to-all(f32[8,1,768]{2,1,0:T(1,128)S(1)} %get-tuple-element.32), channel_id=1, replica_groups=mesh['z'=8,'x'=4,'c'=2,'y'=8] {'z'}, dimensions={0} | all-to-all | bytes 49152 | tf_op jit(solution)/shard_map/all_to_all | solution.py:370
  87.6 0.7 suffix.1
  88.4 0.0 copy-start.4
  88.4 7.3 %all-to-all-start.5 = ((f32[64,1,768]{2,1,0:T(1,128)}), f32[64,1,768]{2,1,0:T(1,128)S(1)}, u32[]{:S(2)}, u32[]{:S(2)}) async-start(f32[64,1,768]{2,1,0:T(1,128)} %suffix.1), calls=%async_computation.5 | async-start | bytes 393216 | tf_op jit(solution)/shard_map/all_to_all | solution.py:360
  95.6 0.0 copy-done.4
  95.7 2.1 %grad.1 = (bf16[5,26,1120]{2,1,0:T(8,128)(2,1)}, f32[5,32,1152]{2,1,0:T(8,128)S(1)}) custom-call(bf16[5,26,1120]{2,1,0:T(8,128)(2,1)S(1)} %bitcast.25, bf16[5,26,1120]{2,1,0:T(8,128)(2,1)S(1)} %bitcast.15, f32[320,128]{1,0:T(8,128)S(1)} %bitcast.23), custom_call_target="tpu_custom_call" | custom-call | tf_op jit(solution)/shard_map/grad/pallas_call | solution.py:327
  97.7 0.0 copy-start.3
  97.7 2.1 %mixed.1 = (bf16[5,26,1120]{2,1,0:T(8,128)(2,1)}, f32[5,32,1152]{2,1,0:T(8,128)S(1)}) custom-call(bf16[5,26,1120]{2,1,0:T(8,128)(2,1)S(1)} %bitcast.20, bf16[5,26,1120]{2,1,0:T(8,128)(2,1)S(1)} %bitcast.16, bf16[2,26,1120]{2,1,0:T(8,128)(2,1)S(1)} %collective-permute-done.above, bf16[2,26,1120]{2,1,0:T(8,128)(2,1)S(1)} %collective-permute-done.1.below, ...), custom_call_target="tpu_custom_call" | custom-call | tf_op jit(solution)/shard_map/mixed/pallas_call | solution.py:327
  99.9 6.6 %all-to-all-done.5 = f32[64,1,768]{2,1,0:T(1,128)S(1)} async-done(((f32[64,1,768]{2,1,0:T(1,128)}), f32[64,1,768]{2,1,0:T(1,128)S(1)}, u32[]{:S(2)}, u32[]{:S(2)}) %all-to-all-start.5) | async-done | bytes 196640 | tf_op jit(solution)/shard_map/all_to_all | solution.py:360
  106.5 0.0 copy-done.3
  106.5 1.5 %key.1 = (bf16[5,26,1120]{2,1,0:T(8,128)(2,1)}, bf16[5,26,1120]{2,1,0:T(8,128)(2,1)}, f32[3,3,1120]{2,1,0:T(4,128)}) custom-call(bf16[5,26,1120]{2,1,0:T(8,128)(2,1)S(1)} %bitcast.27, bf16[5,26,1120]{2,1,0:T(8,128)(2,1)S(1)} %bitcast.21, f32[384,128]{1,0:T(8,128)S(1)} %bitcast.28, f32[5,32,1152]{2,1,0:T(8,128)S(1)} %get-tuple-element.43.refs_3_), custom_call_target="tpu_custom_call" | custom-call | tf_op jit(solution)/shard_map/key/pallas_call | solution.py:327
  (4 shorter events, 0.1 us)
Async XLA Ops:
  0.6 14.0 %copy-start = (bf16[1,5,26,1120]{3,2,1,0:T(8,128)(2,1)S(1)}, bf16[1,5,26,1120]{3,2,1,0:T(8,128)(2,1)}, u32[]{:S(2)}) copy-start(bf16[1,5,26,1120]{3,2,1,0:T(8,128)(2,1)} %param.8) | copy-start | bytes 873604
  0.6 14.0 %copy-start.1 = (bf16[1,5,26,1120]{3,2,1,0:T(8,128)(2,1)S(1)}, bf16[1,5,26,1120]{3,2,1,0:T(8,128)(2,1)}, u32[]{:S(2)}) copy-start(bf16[1,5,26,1120]{3,2,1,0:T(8,128)(2,1)} %param.7) | copy-start | bytes 873604
  3.0 22.0 %all-to-all-start = ((f32[64,1,640]{2,1,0:T(1,128)}), f32[64,1,640]{2,1,0:T(1,128)S(1)}, u32[]{:S(2)}, u32[]{:S(2)}) async-start(f32[64,1,640]{2,1,0:T(1,128)} %bitcast.4), calls=%async_computation | async-start | bytes 327680 | tf_op jit(solution)/shard_map/all_to_all | solution.py:360
  14.7 21.0 %collective-permute-start = (bf16[2,26,1120]{2,1,0:T(8,128)(2,1)S(1)}, bf16[2,26,1120]{2,1,0:T(8,128)(2,1)S(1)}, u32[]{:S(2)}, u32[]{:S(2)}) collective-permute-start(bf16[2,26,1120]{2,1,0:T(8,128)(2,1)S(1)} %get-tuple-element.27), channel_id=1, source_target_pairs={{0,1},{1,2},{2,3},{3,4},{4,5},{5,6},{6,7},{8,9},{9,10},{10,11},{11... | collective-permute-start | bytes 349448 | tf_op jit(solution)/shard_map/ppermute | solution.py:379
  18.0 18.4 %collective-permute-start.1 = (bf16[2,26,1120]{2,1,0:T(8,128)(2,1)S(1)}, bf16[2,26,1120]{2,1,0:T(8,128)(2,1)S(1)}, u32[]{:S(2)}, u32[]{:S(2)}) collective-permute-start(bf16[2,26,1120]{2,1,0:T(8,128)(2,1)S(1)} %get-tuple-element.28), channel_id=1, source_target_pairs={{1,0},{2,1},{3,2},{4,3},{5,4},{6,5},{7,6},{9,8},{10,9},{11,10},{12... | collective-permute-start | bytes 349448 | tf_op jit(solution)/shard_map/ppermute | solution.py:380
  25.6 16.7 %all-to-all-start.1 = ((f32[8,1,640]{2,1,0:T(1,128)}), f32[8,1,640]{2,1,0:T(1,128)S(1)}, u32[]{:S(2)}, u32[]{:S(2)}) async-start(f32[8,1,640]{2,1,0:T(1,128)} %get-tuple-element.26), calls=%async_computation.1 | async-start | bytes 40960 | tf_op jit(solution)/shard_map/all_to_all | solution.py:370
  36.4 24.6 %copy-start.2 = (bf16[1,5,26,1120]{3,2,1,0:T(8,128)(2,1)S(1)}, bf16[1,5,26,1120]{3,2,1,0:T(8,128)(2,1)}, u32[]{:S(2)}) copy-start(bf16[1,5,26,1120]{3,2,1,0:T(8,128)(2,1)} %param.5) | copy-start | bytes 873604
  88.4 7.3 %copy-start.4 = (f32[3,3,1120]{2,1,0:T(4,128)S(1)}, f32[3,3,1120]{2,1,0:T(4,128)}, u32[]{:S(2)}) copy-start(f32[3,3,1120]{2,1,0:T(4,128)} %param.9) | copy-start | bytes 120964
  88.4 18.1 %all-to-all-start.5 = ((f32[64,1,768]{2,1,0:T(1,128)}), f32[64,1,768]{2,1,0:T(1,128)S(1)}, u32[]{:S(2)}, u32[]{:S(2)}) async-start(f32[64,1,768]{2,1,0:T(1,128)} %suffix.1), calls=%async_computation.5 | async-start | bytes 393216 | tf_op jit(solution)/shard_map/all_to_all | solution.py:360
  97.7 8.7 %copy-start.3 = (bf16[1,5,26,1120]{3,2,1,0:T(8,128)(2,1)S(1)}, bf16[1,5,26,1120]{3,2,1,0:T(8,128)(2,1)}, u32[]{:S(2)}) copy-start(bf16[1,5,26,1120]{3,2,1,0:T(8,128)(2,1)} %param.6) | copy-start | bytes 873604

commit v4 on v3

--- a/solution.py
+++ b/solution.py
@@ -14,7 +14,7 @@
 WIDTH = HEADS * HEAD_DIM
 GROUPS = -(-WIDTH // LANES)
 PAD = 32
-BATCH = 3
+BATCH = 5
 STATE_ROWS = GROUPS * HEAD_DIM
 TAIL_ROW = STATE_ROWS + 8 * GROUPS
 

time: 108 us -> 108 us (level)
  no operation moved by 1% of the time
where the time goes in v4:
time: 108 us
  blocking collectives  44 us (41%)
  starting transfers between devices  33.5 us (31%)
  waiting for transfers between devices  18.3 us (17%)
  Pallas kernels  11.4 us (11%)
    all_to_all x2, blocking collectives, exchange(): return lax.all_to_all(x, ('x', 'c', 'y'), 0, 0, tiled=True)  34.8 us
    all_to_all x2, starting transfers between devices, exchange(): return lax.all_to_all(x, ('x', 'c', 'y'), 0, 0, tiled=True)  18.9 us
    all_to_all x2, waiting for transfers between devices, exchange(): return lax.all_to_all(x, ('x', 'c', 'y'), 0, 0, tiled=True)  12.4 us
    pallas_call x11, Pallas kernels, run(): pl.pallas_call(body, out_shape=[a if n in keep else pltpu.VMEM(a.shape, a...  11.4 us
    all_to_all x1, starting transfers between devices, gather(): gathered = lax.all_to_all(whole, 'z', 0, 0, tiled=True)  10 us
    all_to_all x1, blocking collectives, gather(): gathered = lax.all_to_all(whole, 'z', 0, 0, tiled=True)  9.15 us
    all_to_all x1, waiting for transfers between devices, gather(): gathered = lax.all_to_all(whole, 'z', 0, 0, tiled=True)  5.86 us
    ppermute x1, starting transfers between devices, shards(): above = lax.ppermute(last, 'y', upward)  3.29 us
  transfers between devices with their start and end apart: 5, of which 3 were waited for; matrix products, arithmetic and copies ran while one was open for 0% of the time, Pallas kernels for 5%

profile of v4, /device:TPU:1, one launch (start us, length us, event | category | flops | bytes accessed | tf_op | source)
XLA Modules:
  0.0 107.9 jit_solution(3465196800711949966)
XLA Ops:
  0.6 0.0 copy-start
  0.6 0.0 copy-start.1
  0.7 2.4 %state.1 = f32[320,128]{1,0:T(8,128)} custom-call(bf16[5,26,1120]{2,1,0:T(8,128)(2,1)} %bitcast.26, bf16[5,26,1120]{2,1,0:T(8,128)(2,1)} %bitcast.17), custom_call_target="tpu_custom_call" | custom-call | tf_op jit(solution)/shard_map/state/pallas_call | solution.py:327
  3.0 11.6 %all-to-all-start = ((f32[64,1,640]{2,1,0:T(1,128)}), f32[64,1,640]{2,1,0:T(1,128)S(1)}, u32[]{:S(2)}, u32[]{:S(2)}) async-start(f32[64,1,640]{2,1,0:T(1,128)} %bitcast.4), calls=%async_computation | async-start | bytes 327680 | tf_op jit(solution)/shard_map/all_to_all | solution.py:360
  14.6 0.0 copy-done
  14.7 0.0 copy-done.1
  14.7 3.3 %collective-permute-start = (bf16[2,26,1120]{2,1,0:T(8,128)(2,1)S(1)}, bf16[2,26,1120]{2,1,0:T(8,128)(2,1)S(1)}, u32[]{:S(2)}, u32[]{:S(2)}) collective-permute-start(bf16[2,26,1120]{2,1,0:T(8,128)(2,1)S(1)} %get-tuple-element.27), channel_id=1, source_target_pairs={{0,1},{1,2},{2,3},{3,4},{4,5},{5,6},{6,7},{8,9},{9,10},{10,11},{11... | collective-permute-start | bytes 349448 | tf_op jit(solution)/shard_map/ppermute | solution.py:379
  18.0 1.3 %collective-permute-start.1 = (bf16[2,26,1120]{2,1,0:T(8,128)(2,1)S(1)}, bf16[2,26,1120]{2,1,0:T(8,128)(2,1)S(1)}, u32[]{:S(2)}, u32[]{:S(2)}) collective-permute-start(bf16[2,26,1120]{2,1,0:T(8,128)(2,1)S(1)} %get-tuple-element.28), channel_id=1, source_target_pairs={{1,0},{2,1},{3,2},{4,3},{5,4},{6,5},{7,6},{9,8},{10,9},{11,10},{12... | collective-permute-start | bytes 349448 | tf_op jit(solution)/shard_map/ppermute | solution.py:380
  19.3 5.7 %all-to-all-done.received = f32[64,1,640]{2,1,0:T(1,128)S(1)} async-done(((f32[64,1,640]{2,1,0:T(1,128)}), f32[64,1,640]{2,1,0:T(1,128)S(1)}, u32[]{:S(2)}, u32[]{:S(2)}) %all-to-all-start) | async-done | bytes 163872 | tf_op jit(solution)/shard_map/all_to_all | solution.py:360
  25.0 0.6 totals.2
  25.6 10.0 %all-to-all-start.1 = ((f32[8,1,640]{2,1,0:T(1,128)}), f32[8,1,640]{2,1,0:T(1,128)S(1)}, u32[]{:S(2)}, u32[]{:S(2)}) async-start(f32[8,1,640]{2,1,0:T(1,128)} %get-tuple-element.26), calls=%async_computation.1 | async-start | bytes 40960 | tf_op jit(solution)/shard_map/all_to_all | solution.py:370
  35.7 0.0 collective-permute-done.above
  35.7 0.8 terms.1
  36.4 0.0 copy-start.2
  36.4 0.0 collective-permute-done.1.below
  36.4 5.9 %all-to-all-done.1.received = f32[8,1,640]{2,1,0:T(1,128)S(1)} async-done(((f32[8,1,640]{2,1,0:T(1,128)}), f32[8,1,640]{2,1,0:T(1,128)S(1)}, u32[]{:S(2)}, u32[]{:S(2)}) %all-to-all-start.1) | async-done | bytes 20512 | tf_op jit(solution)/shard_map/all_to_all | solution.py:370
  42.3 18.7 %all_to_all.30 = f32[64,1,640]{2,1,0:T(1,128)S(1)} all-to-all(f32[64,1,640]{2,1,0:T(1,128)S(1)} %prefix.1), channel_id=1, replica_groups=mesh['z'=8,'x'=4,'c'=2,'y'=8] {'x','c','y'}, dimensions={0} | all-to-all | bytes 327680 | tf_op jit(solution)/shard_map/all_to_all | solution.py:360
  61.0 0.0 copy-done.2
  61.0 1.2 %query.1 = f32[384,128]{1,0:T(8,128)S(1)} custom-call(bf16[5,26,1120]{2,1,0:T(8,128)(2,1)S(1)} %bitcast.24, bf16[5,26,1120]{2,1,0:T(8,128)(2,1)S(1)} %bitcast.14, f32[320,128]{1,0:T(8,128)S(1)} %bitcast.22, f32[16,1152]{1,0:T(8,128)S(1)} %terms.1), custom_call_target="tpu_custom_call" | custom-call | tf_op jit(solution)/shard_map/query/pallas_call | solution.py:327
  62.2 16.2 %all_to_all.31.received = f32[64,1,768]{2,1,0:T(1,128)S(1)} all-to-all(f32[64,1,768]{2,1,0:T(1,128)S(1)} %bitcast.29), channel_id=1, replica_groups=mesh['z'=8,'x'=4,'c'=2,'y'=8] {'x','c','y'}, dimensions={0} | all-to-all | bytes 393216 | tf_op jit(solution)/shard_map/all_to_all | solution.py:360
  78.4 9.1 %all_to_all.32.received = f32[8,1,768]{2,1,0:T(1,128)S(1)} all-to-all(f32[8,1,768]{2,1,0:T(1,128)S(1)} %get-tuple-element.32), channel_id=1, replica_groups=mesh['z'=8,'x'=4,'c'=2,'y'=8] {'z'}, dimensions={0} | all-to-all | bytes 49152 | tf_op jit(solution)/shard_map/all_to_all | solution.py:370
  87.5 0.7 suffix.1
  88.3 0.0 copy-start.4
  88.3 7.3 %all-to-all-start.5 = ((f32[64,1,768]{2,1,0:T(1,128)}), f32[64,1,768]{2,1,0:T(1,128)S(1)}, u32[]{:S(2)}, u32[]{:S(2)}) async-start(f32[64,1,768]{2,1,0:T(1,128)} %suffix.1), calls=%async_computation.5 | async-start | bytes 393216 | tf_op jit(solution)/shard_map/all_to_all | solution.py:360
  95.5 0.0 copy-done.4
  95.6 2.0 %grad.1 = (bf16[5,26,1120]{2,1,0:T(8,128)(2,1)}, f32[5,32,1152]{2,1,0:T(8,128)S(1)}) custom-call(bf16[5,26,1120]{2,1,0:T(8,128)(2,1)S(1)} %bitcast.25, bf16[5,26,1120]{2,1,0:T(8,128)(2,1)S(1)} %bitcast.15, f32[320,128]{1,0:T(8,128)S(1)} %bitcast.23), custom_call_target="tpu_custom_call" | custom-call | tf_op jit(solution)/shard_map/grad/pallas_call | solution.py:327
  97.6 0.0 copy-start.3
  97.6 2.1 %mixed.1 = (bf16[5,26,1120]{2,1,0:T(8,128)(2,1)}, f32[5,32,1152]{2,1,0:T(8,128)S(1)}) custom-call(bf16[5,26,1120]{2,1,0:T(8,128)(2,1)S(1)} %bitcast.20, bf16[5,26,1120]{2,1,0:T(8,128)(2,1)S(1)} %bitcast.16, bf16[2,26,1120]{2,1,0:T(8,128)(2,1)S(1)} %collective-permute-done.above, bf16[2,26,1120]{2,1,0:T(8,128)(2,1)S(1)} %collective-permute-done.1.below, ...), custom_call_target="tpu_custom_call" | custom-call | tf_op jit(solution)/shard_map/mixed/pallas_call | solution.py:327
  99.7 6.7 %all-to-all-done.5 = f32[64,1,768]{2,1,0:T(1,128)S(1)} async-done(((f32[64,1,768]{2,1,0:T(1,128)}), f32[64,1,768]{2,1,0:T(1,128)S(1)}, u32[]{:S(2)}, u32[]{:S(2)}) %all-to-all-start.5) | async-done | bytes 196640 | tf_op jit(solution)/shard_map/all_to_all | solution.py:360
  106.4 0.0 copy-done.3
  106.4 1.5 %key.1 = (bf16[5,26,1120]{2,1,0:T(8,128)(2,1)}, bf16[5,26,1120]{2,1,0:T(8,128)(2,1)}, f32[3,3,1120]{2,1,0:T(4,128)}) custom-call(bf16[5,26,1120]{2,1,0:T(8,128)(2,1)S(1)} %bitcast.27, bf16[5,26,1120]{2,1,0:T(8,128)(2,1)S(1)} %bitcast.21, f32[384,128]{1,0:T(8,128)S(1)} %bitcast.28, f32[5,32,1152]{2,1,0:T(8,128)S(1)} %get-tuple-element.43.refs_3_), custom_call_target="tpu_custom_call" | custom-call | tf_op jit(solution)/shard_map/key/pallas_call | solution.py:327
  (4 shorter events, 0.1 us)
Async XLA Ops:
  0.6 14.0 %copy-start = (bf16[1,5,26,1120]{3,2,1,0:T(8,128)(2,1)S(1)}, bf16[1,5,26,1120]{3,2,1,0:T(8,128)(2,1)}, u32[]{:S(2)}) copy-start(bf16[1,5,26,1120]{3,2,1,0:T(8,128)(2,1)} %param.8) | copy-start | bytes 873604
  0.6 14.0 %copy-start.1 = (bf16[1,5,26,1120]{3,2,1,0:T(8,128)(2,1)S(1)}, bf16[1,5,26,1120]{3,2,1,0:T(8,128)(2,1)}, u32[]{:S(2)}) copy-start(bf16[1,5,26,1120]{3,2,1,0:T(8,128)(2,1)} %param.7) | copy-start | bytes 873604
  3.0 22.0 %all-to-all-start = ((f32[64,1,640]{2,1,0:T(1,128)}), f32[64,1,640]{2,1,0:T(1,128)S(1)}, u32[]{:S(2)}, u32[]{:S(2)}) async-start(f32[64,1,640]{2,1,0:T(1,128)} %bitcast.4), calls=%async_computation | async-start | bytes 327680 | tf_op jit(solution)/shard_map/all_to_all | solution.py:360
  14.7 21.0 %collective-permute-start = (bf16[2,26,1120]{2,1,0:T(8,128)(2,1)S(1)}, bf16[2,26,1120]{2,1,0:T(8,128)(2,1)S(1)}, u32[]{:S(2)}, u32[]{:S(2)}) collective-permute-start(bf16[2,26,1120]{2,1,0:T(8,128)(2,1)S(1)} %get-tuple-element.27), channel_id=1, source_target_pairs={{0,1},{1,2},{2,3},{3,4},{4,5},{5,6},{6,7},{8,9},{9,10},{10,11},{11... | collective-permute-start | bytes 349448 | tf_op jit(solution)/shard_map/ppermute | solution.py:379
  18.0 18.4 %collective-permute-start.1 = (bf16[2,26,1120]{2,1,0:T(8,128)(2,1)S(1)}, bf16[2,26,1120]{2,1,0:T(8,128)(2,1)S(1)}, u32[]{:S(2)}, u32[]{:S(2)}) collective-permute-start(bf16[2,26,1120]{2,1,0:T(8,128)(2,1)S(1)} %get-tuple-element.28), channel_id=1, source_target_pairs={{1,0},{2,1},{3,2},{4,3},{5,4},{6,5},{7,6},{9,8},{10,9},{11,10},{12... | collective-permute-start | bytes 349448 | tf_op jit(solution)/shard_map/ppermute | solution.py:380
  25.6 16.7 %all-to-all-start.1 = ((f32[8,1,640]{2,1,0:T(1,128)}), f32[8,1,640]{2,1,0:T(1,128)S(1)}, u32[]{:S(2)}, u32[]{:S(2)}) async-start(f32[8,1,640]{2,1,0:T(1,128)} %get-tuple-element.26), calls=%async_computation.1 | async-start | bytes 40960 | tf_op jit(solution)/shard_map/all_to_all | solution.py:370
  36.4 24.6 %copy-start.2 = (bf16[1,5,26,1120]{3,2,1,0:T(8,128)(2,1)S(1)}, bf16[1,5,26,1120]{3,2,1,0:T(8,128)(2,1)}, u32[]{:S(2)}) copy-start(bf16[1,5,26,1120]{3,2,1,0:T(8,128)(2,1)} %param.5) | copy-start | bytes 873604
  88.3 7.3 %copy-start.4 = (f32[3,3,1120]{2,1,0:T(4,128)S(1)}, f32[3,3,1120]{2,1,0:T(4,128)}, u32[]{:S(2)}) copy-start(f32[3,3,1120]{2,1,0:T(4,128)} %param.9) | copy-start | bytes 120964
  88.3 18.1 %all-to-all-start.5 = ((f32[64,1,768]{2,1,0:T(1,128)}), f32[64,1,768]{2,1,0:T(1,128)S(1)}, u32[]{:S(2)}, u32[]{:S(2)}) async-start(f32[64,1,768]{2,1,0:T(1,128)} %suffix.1), calls=%async_computation.5 | async-start | bytes 393216 | tf_op jit(solution)/shard_map/all_to_all | solution.py:360
  97.6 8.8 %copy-start.3 = (bf16[1,5,26,1120]{3,2,1,0:T(8,128)(2,1)S(1)}, bf16[1,5,26,1120]{3,2,1,0:T(8,128)(2,1)}, u32[]{:S(2)}) copy-start(bf16[1,5,26,1120]{3,2,1,0:T(8,128)(2,1)} %param.6) | copy-start | bytes 873604

commit v5 on v4

--- a/solution.py
+++ b/solution.py
@@ -132,9 +132,9 @@
     bands = received.shape[0] // count
     whole = jnp.zeros(received.shape[1:], f32)
     for frame in range(count):
-        total = received[frame * bands]
+        total = received[frame]
         for band in range(1, bands):
-            total = total + received[frame * bands + band]
+            total = total + received[band * count + frame]
         frames[frame] = total
         whole = whole + total
     for n in range(send.shape[0]):
@@ -151,7 +151,7 @@
     for frame in range(count):
         total = total + frames[frame]
         for band in range(bands):
-            send[frame * bands + band] = total
+            send[band * count + frame] = total
 
 
 def suffix_kernel(received, frames, send):
@@ -162,7 +162,7 @@
         later = later + jnp.where(n > plane, received[n], 0.0)
         whole = whole + received[n]
     lane = lax.broadcasted_iota(jnp.int32, received.shape[1:], 1)
-    first = lax.axis_index(("x", "c", "y")) * (received.shape[2] // LANES)
+    first = lax.axis_index(("y", "x", "c")) * (received.shape[2] // LANES)
     row = first + lane // LANES
     norm = jnp.logical_and(row < TAIL_ROW, (row - STATE_ROWS) % 8 == 0)
     summed = jnp.logical_and(row >= STATE_ROWS, jnp.logical_not(norm))
@@ -172,7 +172,7 @@
         later = later + frames[frame]
         out = jnp.where(summed, whole, later)
         for band in range(bands):
-            send[frame * bands + band] = out
+            send[band * count + frame] = out
 
 
 def fill_rim(scratch, ref, above, below=None):
@@ -357,7 +357,7 @@
         return shape((-(-rows_used // peers) * peers, LANES), f32)
 
     def exchange(x):
-        return lax.all_to_all(x, ("x", "c", "y"), 0, 0, tiled=True)
+        return lax.all_to_all(x, ("y", "x", "c"), 0, 0, tiled=True)
 
     def scatter(send):
         return exchange(send.reshape(peers, 1, -1))

time: 108 us -> 109 us (level)
  waiting for transfers between devices: 18.3 us -> 20.9 us
  starting transfers between devices: 33.5 us -> 32 us
    all_to_all x2, waiting for transfers between devices: 12.4 us -> 15.1 us  [exchange(): return lax.all_to_all(x, ('y', 'x', 'c'), 0, 0, tiled=True)]
    all_to_all x2, starting transfers between devices: 18.9 us -> 17.4 us  [exchange(): return lax.all_to_all(x, ('y', 'x', 'c'), 0, 0, tiled=True)]
where the time goes in v5:
time: 109 us
  blocking collectives  43.7 us (40%)
  starting transfers between devices  32 us (29%)
  waiting for transfers between devices  20.9 us (19%)
  Pallas kernels  11.4 us (10%)
    all_to_all x2, blocking collectives, exchange(): return lax.all_to_all(x, ('y', 'x', 'c'), 0, 0, tiled=True)  34.6 us
    all_to_all x2, starting transfers between devices, exchange(): return lax.all_to_all(x, ('y', 'x', 'c'), 0, 0, tiled=True)  17.4 us
    all_to_all x2, waiting for transfers between devices, exchange(): return lax.all_to_all(x, ('y', 'x', 'c'), 0, 0, tiled=True)  15.1 us
    pallas_call x11, Pallas kernels, run(): pl.pallas_call(body, out_shape=[a if n in keep else pltpu.VMEM(a.shape, a...  11.4 us
    all_to_all x1, starting transfers between devices, gather(): gathered = lax.all_to_all(whole, 'z', 0, 0, tiled=True)  10 us
    all_to_all x1, blocking collectives, gather(): gathered = lax.all_to_all(whole, 'z', 0, 0, tiled=True)  9.15 us
    all_to_all x1, waiting for transfers between devices, gather(): gathered = lax.all_to_all(whole, 'z', 0, 0, tiled=True)  5.86 us
    ppermute x1, starting transfers between devices, shards(): above = lax.ppermute(last, 'y', upward)  3.3 us
  transfers between devices with their start and end apart: 5, of which 3 were waited for; matrix products, arithmetic and copies ran while one was open for 0% of the time, Pallas kernels for 5%

profile of v5, /device:TPU:1, one launch (start us, length us, event | category | flops | bytes accessed | tf_op | source)
XLA Modules:
  0.0 108.8 jit_solution(5197134142860876762)
XLA Ops:
  0.6 0.0 copy-start
  0.6 0.0 copy-start.1
  0.7 2.4 %state.1 = f32[320,128]{1,0:T(8,128)} custom-call(bf16[5,26,1120]{2,1,0:T(8,128)(2,1)} %bitcast.26, bf16[5,26,1120]{2,1,0:T(8,128)(2,1)} %bitcast.17), custom_call_target="tpu_custom_call" | custom-call | tf_op jit(solution)/shard_map/state/pallas_call | solution.py:327
  3.0 11.6 %all-to-all-start = ((f32[64,1,640]{2,1,0:T(1,128)}), f32[64,1,640]{2,1,0:T(1,128)S(1)}, u32[]{:S(2)}, u32[]{:S(2)}) async-start(f32[64,1,640]{2,1,0:T(1,128)} %bitcast.4), calls=%async_computation | async-start | bytes 327680 | tf_op jit(solution)/shard_map/all_to_all | solution.py:360
  14.6 0.0 copy-done
  14.6 0.0 copy-done.1
  14.7 3.3 %collective-permute-start = (bf16[2,26,1120]{2,1,0:T(8,128)(2,1)S(1)}, bf16[2,26,1120]{2,1,0:T(8,128)(2,1)S(1)}, u32[]{:S(2)}, u32[]{:S(2)}) collective-permute-start(bf16[2,26,1120]{2,1,0:T(8,128)(2,1)S(1)} %get-tuple-element.27), channel_id=1, source_target_pairs={{0,1},{1,2},{2,3},{3,4},{4,5},{5,6},{6,7},{8,9},{9,10},{10,11},{11... | collective-permute-start | bytes 349448 | tf_op jit(solution)/shard_map/ppermute | solution.py:379
  18.0 1.3 %collective-permute-start.1 = (bf16[2,26,1120]{2,1,0:T(8,128)(2,1)S(1)}, bf16[2,26,1120]{2,1,0:T(8,128)(2,1)S(1)}, u32[]{:S(2)}, u32[]{:S(2)}) collective-permute-start(bf16[2,26,1120]{2,1,0:T(8,128)(2,1)S(1)} %get-tuple-element.28), channel_id=1, source_target_pairs={{1,0},{2,1},{3,2},{4,3},{5,4},{6,5},{7,6},{9,8},{10,9},{11,10},{12... | collective-permute-start | bytes 349448 | tf_op jit(solution)/shard_map/ppermute | solution.py:380
  19.3 7.0 %all-to-all-done.received = f32[64,1,640]{2,1,0:T(1,128)S(1)} async-done(((f32[64,1,640]{2,1,0:T(1,128)}), f32[64,1,640]{2,1,0:T(1,128)S(1)}, u32[]{:S(2)}, u32[]{:S(2)}) %all-to-all-start) | async-done | bytes 163872 | tf_op jit(solution)/shard_map/all_to_all | solution.py:360
  26.3 0.6 totals.2
  27.0 10.0 %all-to-all-start.1 = ((f32[8,1,640]{2,1,0:T(1,128)}), f32[8,1,640]{2,1,0:T(1,128)S(1)}, u32[]{:S(2)}, u32[]{:S(2)}) async-start(f32[8,1,640]{2,1,0:T(1,128)} %get-tuple-element.26), calls=%async_computation.1 | async-start | bytes 40960 | tf_op jit(solution)/shard_map/all_to_all | solution.py:370
  37.0 0.0 collective-permute-done.above
  37.0 0.8 terms.1
  37.8 0.0 copy-start.2
  37.8 0.0 collective-permute-done.1.below
  37.8 5.9 %all-to-all-done.1.received = f32[8,1,640]{2,1,0:T(1,128)S(1)} async-done(((f32[8,1,640]{2,1,0:T(1,128)}), f32[8,1,640]{2,1,0:T(1,128)S(1)}, u32[]{:S(2)}, u32[]{:S(2)}) %all-to-all-start.1) | async-done | bytes 20512 | tf_op jit(solution)/shard_map/all_to_all | solution.py:370
  43.7 18.7 %all_to_all.30 = f32[64,1,640]{2,1,0:T(1,128)S(1)} all-to-all(f32[64,1,640]{2,1,0:T(1,128)S(1)} %prefix.1), channel_id=1, replica_groups=mesh['z'=8,'x'=4,'c'=2,'y'=8] {'y','x','c'}, dimensions={0} | all-to-all | bytes 327680 | tf_op jit(solution)/shard_map/all_to_all | solution.py:360
  62.3 0.0 copy-done.2
  62.3 1.2 %query.1 = f32[384,128]{1,0:T(8,128)S(1)} custom-call(bf16[5,26,1120]{2,1,0:T(8,128)(2,1)S(1)} %bitcast.24, bf16[5,26,1120]{2,1,0:T(8,128)(2,1)S(1)} %bitcast.14, f32[320,128]{1,0:T(8,128)S(1)} %bitcast.22, f32[16,1152]{1,0:T(8,128)S(1)} %terms.1), custom_call_target="tpu_custom_call" | custom-call | tf_op jit(solution)/shard_map/query/pallas_call | solution.py:327
  63.5 15.9 %all_to_all.31.received = f32[64,1,768]{2,1,0:T(1,128)S(1)} all-to-all(f32[64,1,768]{2,1,0:T(1,128)S(1)} %bitcast.29), channel_id=1, replica_groups=mesh['z'=8,'x'=4,'c'=2,'y'=8] {'y','x','c'}, dimensions={0} | all-to-all | bytes 393216 | tf_op jit(solution)/shard_map/all_to_all | solution.py:360
  79.5 9.1 %all_to_all.32.received = f32[8,1,768]{2,1,0:T(1,128)S(1)} all-to-all(f32[8,1,768]{2,1,0:T(1,128)S(1)} %get-tuple-element.32), channel_id=1, replica_groups=mesh['z'=8,'x'=4,'c'=2,'y'=8] {'z'}, dimensions={0} | all-to-all | bytes 49152 | tf_op jit(solution)/shard_map/all_to_all | solution.py:370
  88.6 0.7 suffix.1
  89.4 0.0 copy-start.4
  89.4 5.7 %all-to-all-start.5 = ((f32[64,1,768]{2,1,0:T(1,128)}), f32[64,1,768]{2,1,0:T(1,128)S(1)}, u32[]{:S(2)}, u32[]{:S(2)}) async-start(f32[64,1,768]{2,1,0:T(1,128)} %suffix.1), calls=%async_computation.5 | async-start | bytes 393216 | tf_op jit(solution)/shard_map/all_to_all | solution.py:360
  95.1 0.0 copy-done.4
  95.2 2.0 %grad.1 = (bf16[5,26,1120]{2,1,0:T(8,128)(2,1)}, f32[5,32,1152]{2,1,0:T(8,128)S(1)}) custom-call(bf16[5,26,1120]{2,1,0:T(8,128)(2,1)S(1)} %bitcast.25, bf16[5,26,1120]{2,1,0:T(8,128)(2,1)S(1)} %bitcast.15, f32[320,128]{1,0:T(8,128)S(1)} %bitcast.23), custom_call_target="tpu_custom_call" | custom-call | tf_op jit(solution)/shard_map/grad/pallas_call | solution.py:327
  97.2 0.0 copy-start.3
  97.2 2.1 %mixed.1 = (bf16[5,26,1120]{2,1,0:T(8,128)(2,1)}, f32[5,32,1152]{2,1,0:T(8,128)S(1)}) custom-call(bf16[5,26,1120]{2,1,0:T(8,128)(2,1)S(1)} %bitcast.20, bf16[5,26,1120]{2,1,0:T(8,128)(2,1)S(1)} %bitcast.16, bf16[2,26,1120]{2,1,0:T(8,128)(2,1)S(1)} %collective-permute-done.above, bf16[2,26,1120]{2,1,0:T(8,128)(2,1)S(1)} %collective-permute-done.1.below, ...), custom_call_target="tpu_custom_call" | custom-call | tf_op jit(solution)/shard_map/mixed/pallas_call | solution.py:327
  99.3 8.0 %all-to-all-done.5 = f32[64,1,768]{2,1,0:T(1,128)S(1)} async-done(((f32[64,1,768]{2,1,0:T(1,128)}), f32[64,1,768]{2,1,0:T(1,128)S(1)}, u32[]{:S(2)}, u32[]{:S(2)}) %all-to-all-start.5) | async-done | bytes 196640 | tf_op jit(solution)/shard_map/all_to_all | solution.py:360
  107.4 0.0 copy-done.3
  107.4 1.5 %key.1 = (bf16[5,26,1120]{2,1,0:T(8,128)(2,1)}, bf16[5,26,1120]{2,1,0:T(8,128)(2,1)}, f32[3,3,1120]{2,1,0:T(4,128)}) custom-call(bf16[5,26,1120]{2,1,0:T(8,128)(2,1)S(1)} %bitcast.27, bf16[5,26,1120]{2,1,0:T(8,128)(2,1)S(1)} %bitcast.21, f32[384,128]{1,0:T(8,128)S(1)} %bitcast.28, f32[5,32,1152]{2,1,0:T(8,128)S(1)} %get-tuple-element.43.refs_3_), custom_call_target="tpu_custom_call" | custom-call | tf_op jit(solution)/shard_map/key/pallas_call | solution.py:327
  (4 shorter events, 0.1 us)
Async XLA Ops:
  0.6 14.0 %copy-start = (bf16[1,5,26,1120]{3,2,1,0:T(8,128)(2,1)S(1)}, bf16[1,5,26,1120]{3,2,1,0:T(8,128)(2,1)}, u32[]{:S(2)}) copy-start(bf16[1,5,26,1120]{3,2,1,0:T(8,128)(2,1)} %param.8) | copy-start | bytes 873604
  0.6 14.0 %copy-start.1 = (bf16[1,5,26,1120]{3,2,1,0:T(8,128)(2,1)S(1)}, bf16[1,5,26,1120]{3,2,1,0:T(8,128)(2,1)}, u32[]{:S(2)}) copy-start(bf16[1,5,26,1120]{3,2,1,0:T(8,128)(2,1)} %param.7) | copy-start | bytes 873604
  3.0 23.3 %all-to-all-start = ((f32[64,1,640]{2,1,0:T(1,128)}), f32[64,1,640]{2,1,0:T(1,128)S(1)}, u32[]{:S(2)}, u32[]{:S(2)}) async-start(f32[64,1,640]{2,1,0:T(1,128)} %bitcast.4), calls=%async_computation | async-start | bytes 327680 | tf_op jit(solution)/shard_map/all_to_all | solution.py:360
  14.7 22.3 %collective-permute-start = (bf16[2,26,1120]{2,1,0:T(8,128)(2,1)S(1)}, bf16[2,26,1120]{2,1,0:T(8,128)(2,1)S(1)}, u32[]{:S(2)}, u32[]{:S(2)}) collective-permute-start(bf16[2,26,1120]{2,1,0:T(8,128)(2,1)S(1)} %get-tuple-element.27), channel_id=1, source_target_pairs={{0,1},{1,2},{2,3},{3,4},{4,5},{5,6},{6,7},{8,9},{9,10},{10,11},{11... | collective-permute-start | bytes 349448 | tf_op jit(solution)/shard_map/ppermute | solution.py:379
  18.0 19.8 %collective-permute-start.1 = (bf16[2,26,1120]{2,1,0:T(8,128)(2,1)S(1)}, bf16[2,26,1120]{2,1,0:T(8,128)(2,1)S(1)}, u32[]{:S(2)}, u32[]{:S(2)}) collective-permute-start(bf16[2,26,1120]{2,1,0:T(8,128)(2,1)S(1)} %get-tuple-element.28), channel_id=1, source_target_pairs={{1,0},{2,1},{3,2},{4,3},{5,4},{6,5},{7,6},{9,8},{10,9},{11,10},{12... | collective-permute-start | bytes 349448 | tf_op jit(solution)/shard_map/ppermute | solution.py:380
  27.0 16.7 %all-to-all-start.1 = ((f32[8,1,640]{2,1,0:T(1,128)}), f32[8,1,640]{2,1,0:T(1,128)S(1)}, u32[]{:S(2)}, u32[]{:S(2)}) async-start(f32[8,1,640]{2,1,0:T(1,128)} %get-tuple-element.26), calls=%async_computation.1 | async-start | bytes 40960 | tf_op jit(solution)/shard_map/all_to_all | solution.py:370
  37.8 24.6 %copy-start.2 = (bf16[1,5,26,1120]{3,2,1,0:T(8,128)(2,1)S(1)}, bf16[1,5,26,1120]{3,2,1,0:T(8,128)(2,1)}, u32[]{:S(2)}) copy-start(bf16[1,5,26,1120]{3,2,1,0:T(8,128)(2,1)} %param.5) | copy-start | bytes 873604
  89.4 5.8 %copy-start.4 = (f32[3,3,1120]{2,1,0:T(4,128)S(1)}, f32[3,3,1120]{2,1,0:T(4,128)}, u32[]{:S(2)}) copy-start(f32[3,3,1120]{2,1,0:T(4,128)} %param.9) | copy-start | bytes 120964
  89.4 18.0 %all-to-all-start.5 = ((f32[64,1,768]{2,1,0:T(1,128)}), f32[64,1,768]{2,1,0:T(1,128)S(1)}, u32[]{:S(2)}, u32[]{:S(2)}) async-start(f32[64,1,768]{2,1,0:T(1,128)} %suffix.1), calls=%async_computation.5 | async-start | bytes 393216 | tf_op jit(solution)/shard_map/all_to_all | solution.py:360
  97.2 10.2 %copy-start.3 = (bf16[1,5,26,1120]{3,2,1,0:T(8,128)(2,1)S(1)}, bf16[1,5,26,1120]{3,2,1,0:T(8,128)(2,1)}, u32[]{:S(2)}) copy-start(bf16[1,5,26,1120]{3,2,1,0:T(8,128)(2,1)} %param.6) | copy-start | bytes 873604
